TPU v7x, 32 devices: a whole 2x2x4 slice. The times are simulated.
32 devices in a mesh: img: 2 (over x), tok: 4 (over z), seq: 4 (over y, core).
Axes of the slice: x: 2, y: 2, z: 4, core: 2. Of those that a mesh axis runs over, the one named last changes fastest.
Arguments:
- images: bfloat16 [2, 64, 64, 768], P('img', ('tok', 'seq')), may hold values from -6 to 6
- teacher: bfloat16 [2, 64, 64, 768], P('img', ('tok', 'seq')), may hold values from -6 to 6
- valid_mask: int32 [2, 64, 64], P('img', ('tok', 'seq')), may hold values from 0 to 1, as said below
- out_grad: bfloat16 [2, 64, 64, 768], P('img', ('tok', 'seq')), may hold values from -6 to 6
- attn_gain: float32 [768], replicated, may hold values from 0.5 to 1.5
- attn_shift: float32 [768], replicated, may hold values from -1 to 1
- qkv_weight: bfloat16 [768, 2304], P('img'), may hold values from -0.21875 to 0.21875
- query_bias: float32 [768], replicated, may hold values from -1 to 1
- value_bias: float32 [768], replicated, may hold values from -1 to 1
- rel_rows: float32 [27, 64], replicated, may hold values from -0.6 to 0.6
- rel_cols: float32 [27, 64], replicated, may hold values from -0.6 to 0.6
- proj_weight: bfloat16 [768, 768], P('img'), may hold values from -0.875 to 0.875
- proj_bias: float32 [768], replicated, may hold values from -1 to 1
- mlp_gain: float32 [768], replicated, may hold values from 0.5 to 1.5
- mlp_shift: float32 [768], replicated, may hold values from -1 to 1
- up_weight: bfloat16 [768, 3072], P('img'), may hold values from -0.21875 to 0.21875
- up_bias: float32 [3072], replicated, may hold values from -1 to 1
- down_weight: bfloat16 [3072, 768], P('img'), may hold values from -0.109375 to 0.109375
- down_bias: float32 [768], replicated, may hold values from -1 to 1
Outputs:
- block_out: bfloat16 [2, 64, 64, 768], P('img', ('tok', 'seq'))
- distill_loss: float32 [], replicated
- images_grad: float32 [2, 64, 64, 768], P('img', ('tok', 'seq'))
- attn_gain_grad: float32 [768], replicated
- attn_shift_grad: float32 [768], replicated
- qkv_weight_grad: float32 [768, 2304], P('img')
- query_bias_grad: float32 [768], replicated
- value_bias_grad: float32 [768], replicated
- rel_rows_grad: float32 [27, 64], replicated
- rel_cols_grad: float32 [27, 64], replicated
- proj_weight_grad: float32 [768, 768], P('img')
- proj_bias_grad: float32 [768], replicated
- mlp_gain_grad: float32 [768], replicated
- mlp_shift_grad: float32 [768], replicated
- up_weight_grad: float32 [768, 3072], P('img')
- up_bias_grad: float32 [3072], replicated
- down_weight_grad: float32 [3072, 768], P('img')
- down_bias_grad: float32 [768], replicated
Inputs may be any that keep to these rules, and one draw needn't show every extreme that they name: `valid_mask`: the first token of every image is valid.
All inputs are finite; a program needn't handle non-finite values.
Results may differ from a plain program's by a relative error of at most 0.012.
Values may be sent and summed in bfloat16 or wider, within the bound.
No kernel may reach another device: no remote copies, remote signals or barrier semaphores. Data moves between devices by JAX's collectives and lax.ppermute only.
A program may use at most 320 MiB of HBM per device.

v0:
```python
import jax
import jax.numpy as jnp
from jax import lax
from jax.sharding import PartitionSpec as P

HD = 64
WIN = 14
H = 64
W = 64


EPS = 1e-06
HIGHEST = lax.Precision.HIGHEST


def shifted(block, axis, distance):
    devices = range(lax.axis_size(axis))
    route = [(i - distance, i) for i in devices if i - distance in devices]
    return lax.ppermute(block, axis, route)


def norm_rows(values, gain, shift):
    centre = jnp.mean(values, axis=-1, keepdims=True)
    centred = values - centre
    spread = jnp.mean(centred * centred, axis=-1, keepdims=True)
    return centred * lax.rsqrt(spread + EPS) * gain + shift


def gelu_exact(values):
    return jax.nn.gelu(values, approximate=False)


def offset_table(window):
    places = jnp.arange(window)
    index_grid = places[:, None] - places[None, :] + window - 1
    return (index_grid[:, :, None] == jnp.arange(2 * window - 1)[None, None, :]).astype(jnp.float32)


def rel_matrix(rel_table, window):
    return jnp.einsum("ikm,mc->ikc", offset_table(window), rel_table, precision=HIGHEST)


def window_scores(queries, keys_win, row_offsets, col_offsets, score_scale):
    direct = jnp.einsum(
        "gaibjhc,gakblhc->gabhijkl", queries, keys_win, preferred_element_type=jnp.float32
    )
    direct = direct * score_scale
    query_wide = queries.astype(jnp.float32)
    along_rows = jnp.einsum("gaibjhc,ikc->gabhijk", query_wide, row_offsets, precision=HIGHEST)
    along_cols = jnp.einsum("gaibjhc,jlc->gabhijl", query_wide, col_offsets, precision=HIGHEST)
    return (direct + along_rows[..., None] + along_cols[..., None, :], query_wide)


def local(
    images,
    teacher,
    valid_mask,
    out_grad,
    attn_gain,
    attn_shift,
    qkv_weight,
    query_bias,
    value_bias,
    rel_rows,
    rel_cols,
    proj_weight,
    proj_bias,
    mlp_gain,
    mlp_shift,
    up_weight,
    up_bias,
    down_weight,
    down_bias,
):
    band_devices = lax.axis_size("tok")
    head_devices = lax.axis_size("seq")
    band_index = lax.axis_index("tok")
    head_index = lax.axis_index("seq")
    batch_here, own_rows, grid_cols, width_model = images.shape
    band_rows = own_rows * head_devices
    margin = (band_rows - WIN) * (band_devices - 1)
    padded_cols = -(-grid_cols // WIN) * WIN
    window_cols = padded_cols // WIN
    slot_rows = 2 * WIN
    spare_rows = max(band_rows + margin, margin + slot_rows)
    local_width = width_model // head_devices
    local_heads = local_width // HD
    score_scale = HD ** (-0.5)
    first_row = margin - (band_rows - WIN) * band_index
    last_band = (band_index == band_devices - 1).astype(jnp.float32)
    slot_weight = jnp.stack([jnp.float32(1.0), last_band])[None, :, None, None, None, None, None]
    row_ids = lax.broadcasted_iota(jnp.int32, (spare_rows, padded_cols), 0)
    col_ids = lax.broadcasted_iota(jnp.int32, (spare_rows, padded_cols), 1)
    real_cells = (row_ids < band_rows + margin) & (col_ids < grid_cols)
    slot_real = lax.dynamic_slice_in_dim(real_cells, first_row, slot_rows, 0)
    row_offsets = rel_matrix(rel_rows, WIN)
    col_offsets = rel_matrix(rel_cols, WIN)
    inputs = images.astype(jnp.float32)
    normed = norm_rows(inputs, attn_gain, attn_shift)
    normed_low = normed.astype(jnp.bfloat16)
    qkv_full, proj_full, up_full, down_full = (
        lax.all_gather(qkv_weight, "img", axis=0, tiled=True),
        lax.all_gather(proj_weight, "img", axis=0, tiled=True),
        lax.all_gather(up_weight, "img", axis=0, tiled=True),
        lax.all_gather(down_weight, "img", axis=0, tiled=True),
    )
    qkv_bias = jnp.concatenate([query_bias, jnp.zeros_like(query_bias), value_bias])
    mixed_qkv = (
        jnp.einsum("grwc,cf->grwf", normed_low, qkv_full, preferred_element_type=jnp.float32)
        + qkv_bias
    )
    mixed_qkv = mixed_qkv.astype(jnp.bfloat16).reshape(
        batch_here, own_rows, grid_cols, 3, head_devices, local_width
    )
    by_heads = lax.all_to_all(mixed_qkv, "seq", split_axis=4, concat_axis=1, tiled=True).reshape(
        batch_here, band_rows, grid_cols, 3, local_width
    )
    below_rows = shifted(by_heads[:, band_rows - margin :], "tok", 1)
    joined_rows = jnp.concatenate([below_rows, by_heads], axis=1)
    pad_token = jnp.stack(
        [
            lax.dynamic_slice_in_dim(query_bias, head_index * local_width, local_width),
            jnp.zeros((local_width,), jnp.float32),
            lax.dynamic_slice_in_dim(value_bias, head_index * local_width, local_width),
        ]
    ).astype(jnp.bfloat16)
    spread_rows = jnp.pad(
        joined_rows,
        (
            (0, 0),
            (0, spare_rows - band_rows - margin),
            (0, padded_cols - grid_cols),
            (0, 0),
            (0, 0),
        ),
    )
    extended = jnp.where(
        real_cells[None, :, :, None, None], spread_rows, pad_token[None, None, None]
    )
    slot_qkv = lax.dynamic_slice_in_dim(extended, first_row, slot_rows, 1)
    windows = slot_qkv.reshape(batch_here, 2, WIN, window_cols, WIN, 3, local_heads, HD)
    queries = windows[:, :, :, :, :, 0]
    keys_win = windows[:, :, :, :, :, 1]
    values = windows[:, :, :, :, :, 2]
    scores, query_wide = window_scores(queries, keys_win, row_offsets, col_offsets, score_scale)
    top_score = jnp.max(scores, axis=(-2, -1), keepdims=True)
    exp_total = jnp.sum(jnp.exp(scores - top_score), axis=(-2, -1), keepdims=True)
    log_total = top_score + jnp.log(exp_total)
    probs_low = jnp.exp(scores - log_total).astype(jnp.bfloat16)
    attended = jnp.einsum(
        "gabhijkl,gakblhc->gaibjhc", probs_low, values, preferred_element_type=jnp.float32
    )
    attended_low = (
        (attended * slot_weight)
        .astype(jnp.bfloat16)
        .reshape(batch_here, slot_rows, padded_cols, local_width)
    )
    placed = lax.dynamic_update_slice_in_dim(
        jnp.zeros((batch_here, spare_rows, padded_cols, local_width), jnp.bfloat16),
        attended_low,
        first_row,
        1,
    )
    placed = placed[:, : band_rows + margin, :grid_cols]
    from_next = shifted(placed[:, :margin], "tok", -1)
    band_out = placed[:, margin:] + jnp.pad(
        from_next, ((0, 0), (band_rows - margin, 0), (0, 0), (0, 0))
    )
    heads_out = lax.all_to_all(band_out, "seq", split_axis=1, concat_axis=3, tiled=True)
    projected = (
        jnp.einsum("grwf,fc->grwc", heads_out, proj_full, preferred_element_type=jnp.float32)
        + proj_bias
    )
    residual = inputs + projected
    normed_two = norm_rows(residual, mlp_gain, mlp_shift).astype(jnp.bfloat16)
    hidden_pre = (
        jnp.einsum("grwc,cm->grwm", normed_two, up_full, preferred_element_type=jnp.float32)
        + up_bias
    )
    hidden = gelu_exact(hidden_pre).astype(jnp.bfloat16)
    result = (
        residual
        + jnp.einsum("grwm,mc->grwc", hidden, down_full, preferred_element_type=jnp.float32)
        + down_bias
    )
    differ = result - teacher.astype(jnp.float32)
    valid_rows = valid_mask.astype(jnp.float32)[..., None]
    squares_here = jnp.sum(valid_rows * differ * differ)
    count_here = jnp.sum(valid_mask.astype(jnp.float32))
    square_total, count_total = lax.psum((squares_here, count_here), ("img", "tok", "seq"))
    distill_loss = square_total / (count_total * width_model)
    tokens_all = batch_here * lax.axis_size("img") * H * W
    result_grad = out_grad.astype(jnp.float32) + valid_rows * differ * (
        tokens_all / (4.0 * count_total)
    )
    qkv_full, proj_full, up_full, down_full = (
        lax.all_gather(qkv_weight, "img", axis=0, tiled=True),
        lax.all_gather(proj_weight, "img", axis=0, tiled=True),
        lax.all_gather(up_weight, "img", axis=0, tiled=True),
        lax.all_gather(down_weight, "img", axis=0, tiled=True),
    )
    down_in = result_grad.astype(jnp.bfloat16)
    down_bias_grad = jnp.sum(down_in.astype(jnp.float32), axis=(0, 1, 2))
    down_grad = jnp.einsum("grwm,grwc->mc", hidden, down_in, preferred_element_type=jnp.float32)
    hidden_grad = jnp.einsum(
        "grwc,mc->grwm", down_in, down_full, preferred_element_type=jnp.float32
    )
    unused_gelu, gelu_back = jax.vjp(gelu_exact, hidden_pre)
    pre_grad = gelu_back(hidden_grad)[0].astype(jnp.bfloat16)
    up_bias_grad = jnp.sum(pre_grad.astype(jnp.float32), axis=(0, 1, 2))
    up_grad = jnp.einsum("grwc,grwm->cm", normed_two, pre_grad, preferred_element_type=jnp.float32)
    normed_two_grad = jnp.einsum(
        "grwm,cm->grwc", pre_grad, up_full, preferred_element_type=jnp.float32
    )
    unused_norm, norm_two_back = jax.vjp(norm_rows, residual, mlp_gain, mlp_shift)
    residual_part, mlp_gain_grad, mlp_shift_grad = norm_two_back(normed_two_grad)
    residual_grad = result_grad + residual_part
    proj_in = residual_grad.astype(jnp.bfloat16)
    proj_bias_grad = jnp.sum(proj_in.astype(jnp.float32), axis=(0, 1, 2))
    proj_grad = jnp.einsum("grwf,grwc->fc", heads_out, proj_in, preferred_element_type=jnp.float32)
    heads_grad = jnp.einsum(
        "grwc,fc->grwf", proj_in, proj_full, preferred_element_type=jnp.float32
    ).astype(jnp.bfloat16)
    band_grad = lax.all_to_all(heads_grad, "seq", split_axis=3, concat_axis=1, tiled=True)
    lower_grad = shifted(band_grad[:, band_rows - margin :], "tok", 1)
    grad_rows = jnp.concatenate([lower_grad, band_grad], axis=1)
    grad_ext = jnp.pad(
        grad_rows,
        ((0, 0), (0, spare_rows - band_rows - margin), (0, padded_cols - grid_cols), (0, 0)),
    )
    grad_slot = lax.dynamic_slice_in_dim(grad_ext, first_row, slot_rows, 1)
    grad_slot = grad_slot.reshape(batch_here, 2, WIN, window_cols, WIN, local_heads, HD)
    grad_slot = (grad_slot.astype(jnp.float32) * slot_weight).astype(jnp.bfloat16)
    scores, query_wide = window_scores(queries, keys_win, row_offsets, col_offsets, score_scale)
    probs = jnp.exp(scores - log_total)
    probs_low = probs.astype(jnp.bfloat16)
    value_grad = jnp.einsum(
        "gabhijkl,gaibjhc->gakblhc", probs_low, grad_slot, preferred_element_type=jnp.float32
    )
    probs_grad = jnp.einsum(
        "gaibjhc,gakblhc->gabhijkl", grad_slot, values, preferred_element_type=jnp.float32
    )
    inner = jnp.sum(probs_grad * probs, axis=(-2, -1), keepdims=True)
    score_grad = (probs * (probs_grad - inner)).astype(jnp.bfloat16)
    query_grad = (
        jnp.einsum(
            "gabhijkl,gakblhc->gaibjhc", score_grad, keys_win, preferred_element_type=jnp.float32
        )
        * score_scale
    )
    key_grad = (
        jnp.einsum(
            "gabhijkl,gaibjhc->gakblhc", score_grad, queries, preferred_element_type=jnp.float32
        )
        * score_scale
    )
    score_wide = score_grad.astype(jnp.float32)
    row_terms = jnp.sum(score_wide, axis=-1)
    col_terms = jnp.sum(score_wide, axis=-2)
    query_grad = query_grad + jnp.einsum(
        "gabhijk,ikc->gaibjhc", row_terms, row_offsets, precision=HIGHEST
    )
    query_grad = query_grad + jnp.einsum(
        "gabhijl,jlc->gaibjhc", col_terms, col_offsets, precision=HIGHEST
    )
    row_offset_grad = jnp.einsum("gabhijk,gaibjhc->ikc", row_terms, query_wide, precision=HIGHEST)
    col_offset_grad = jnp.einsum("gabhijl,gaibjhc->jlc", col_terms, query_wide, precision=HIGHEST)
    rel_rows_grad = jnp.einsum("ikm,ikc->mc", offset_table(WIN), row_offset_grad, precision=HIGHEST)
    rel_cols_grad = jnp.einsum("ikm,ikc->mc", offset_table(WIN), col_offset_grad, precision=HIGHEST)
    slot_grad = jnp.stack([query_grad, key_grad, value_grad], axis=5).astype(jnp.bfloat16)
    slot_grad = slot_grad.reshape(batch_here, slot_rows, padded_cols, 3, local_width)
    pad_grad = jnp.sum(
        jnp.where(slot_real[None, :, :, None, None], 0.0, slot_grad.astype(jnp.float32)),
        axis=(0, 1, 2),
    )
    placed_grad = lax.dynamic_update_slice_in_dim(
        jnp.zeros((batch_here, spare_rows, padded_cols, 3, local_width), jnp.bfloat16),
        slot_grad,
        first_row,
        1,
    )
    placed_grad = placed_grad[:, : band_rows + margin, :grid_cols]
    upper_grad = shifted(placed_grad[:, :margin], "tok", -1)
    own_grad = placed_grad[:, margin:] + jnp.pad(
        upper_grad, ((0, 0), (band_rows - margin, 0), (0, 0), (0, 0), (0, 0))
    )
    own_grad = own_grad.reshape(batch_here, band_rows, grid_cols, 3, 1, local_width)
    token_grad = lax.all_to_all(own_grad, "seq", split_axis=1, concat_axis=4, tiled=True)
    token_grad = token_grad.reshape(batch_here, own_rows, grid_cols, 3 * width_model)
    qkv_sums = jnp.sum(token_grad.astype(jnp.float32), axis=(0, 1, 2)).reshape(3, width_model)
    empty_width = jnp.zeros((width_model,), jnp.float32)
    query_bias_grad = qkv_sums[0] + lax.dynamic_update_slice_in_dim(
        empty_width, pad_grad[0], head_index * local_width, 0
    )
    value_bias_grad = qkv_sums[2] + lax.dynamic_update_slice_in_dim(
        empty_width, pad_grad[2], head_index * local_width, 0
    )
    qkv_grad = jnp.einsum(
        "grwc,grwf->cf", normed_low, token_grad, preferred_element_type=jnp.float32
    )
    normed_grad = jnp.einsum(
        "grwf,cf->grwc", token_grad, qkv_full, preferred_element_type=jnp.float32
    )
    unused_first, norm_one_back = jax.vjp(norm_rows, inputs, attn_gain, attn_shift)
    input_part, attn_gain_grad, attn_shift_grad = norm_one_back(normed_grad)
    images_grad = residual_grad + input_part
    flat_sums = (
        lax.psum_scatter(
            qkv_grad.reshape(-1), ("img", "tok", "seq"), scatter_dimension=0, tiled=True
        ),
        lax.psum_scatter(
            proj_grad.reshape(-1), ("img", "tok", "seq"), scatter_dimension=0, tiled=True
        ),
        lax.psum_scatter(
            up_grad.reshape(-1), ("img", "tok", "seq"), scatter_dimension=0, tiled=True
        ),
        lax.psum_scatter(
            down_grad.reshape(-1), ("img", "tok", "seq"), scatter_dimension=0, tiled=True
        ),
    )
    flat_parts = (
        lax.all_gather(
            flat_sums[0].astype(jnp.bfloat16), ("tok", "seq"), axis=0, tiled=True
        ).astype(jnp.float32),
        lax.all_gather(
            flat_sums[1].astype(jnp.bfloat16), ("tok", "seq"), axis=0, tiled=True
        ).astype(jnp.float32),
        lax.all_gather(
            flat_sums[2].astype(jnp.bfloat16), ("tok", "seq"), axis=0, tiled=True
        ).astype(jnp.float32),
        lax.all_gather(
            flat_sums[3].astype(jnp.bfloat16), ("tok", "seq"), axis=0, tiled=True
        ).astype(jnp.float32),
    )
    small_sums = lax.psum(
        (
            attn_gain_grad,
            attn_shift_grad,
            query_bias_grad,
            value_bias_grad,
            rel_rows_grad,
            rel_cols_grad,
            proj_bias_grad,
            mlp_gain_grad,
            mlp_shift_grad,
            up_bias_grad,
            down_bias_grad,
        ),
        ("img", "tok", "seq"),
    )
    qkv_weight_grad = flat_parts[0].reshape(-1, 3 * width_model)
    proj_weight_grad = flat_parts[1].reshape(-1, width_model)
    up_weight_grad = flat_parts[2].reshape(-1, up_full.shape[1])
    down_weight_grad = flat_parts[3].reshape(-1, width_model)
    return (
        result.astype(jnp.bfloat16),
        distill_loss,
        images_grad,
        small_sums[0],
        small_sums[1],
        qkv_weight_grad,
        small_sums[2],
        small_sums[3],
        small_sums[4],
        small_sums[5],
        proj_weight_grad,
        small_sums[6],
        small_sums[7],
        small_sums[8],
        up_weight_grad,
        small_sums[9],
        down_weight_grad,
        small_sums[10],
    )


def solution(mesh):
    return jax.shard_map(
        local,
        mesh=mesh,
        in_specs=(
            P("img", ("tok", "seq"), None, None),
            P("img", ("tok", "seq"), None, None),
            P("img", ("tok", "seq"), None),
            P("img", ("tok", "seq"), None, None),
            P(),
            P(),
            P("img", None),
            P(),
            P(),
            P(),
            P(),
            P("img", None),
            P(),
            P(),
            P(),
            P("img", None),
            P(),
            P("img", None),
            P(),
        ),
        out_specs=(
            P("img", ("tok", "seq"), None, None),
            P(),
            P("img", ("tok", "seq"), None, None),
            P(),
            P(),
            P("img", None),
            P(),
            P(),
            P(),
            P(),
            P("img", None),
            P(),
            P(),
            P(),
            P("img", None),
            P(),
            P("img", None),
            P(),
        ),
        check_vma=False,
    )
```

profile of v0, /device:TPU:0, one launch (start us, length us, event | category | flops | bytes accessed | tf_op | source)
XLA Modules:
  0.0 1224.8 jit_solution(18022483437319934143)
XLA Ops:
  10.8 50.9 %all-gather.8.cloned.1.call-done = bf16[768,2304]{1,0:T(8,128)(2,1)} async-done(((bf16[384,2304]{1,0:T(8,128)(2,1)}), bf16[768,2304]{1,0:T(8,128)(2,1)}) %all-gather.8.cloned.1.call-update) | async-done | bytes 3538960 | tf_op jit(solution)/shard_map/all_gather | solution.py:102
  72.7 18.9 %all-to-all-done = bf16[1,4,64,3,4,192]{5,2,3,1,0,4:T(8,128)(2,1)S(1)} async-done(((bf16[1,4,64,3,4,192]{5,2,3,1,0,4:T(8,128)(2,1)}), bf16[1,4,64,3,4,192]{5,2,3,1,0,4:T(8,128)(2,1)S(1)}, u32[]{:S(2)}, u32[]{:S(2)}) %all-to-all-start) | async-done | bytes 1179680 | tf_op jit(solution)/shard_map/all_to_all | solution.py:115
  96.1 11.4 collective-permute-done
  122.5 13.9 %convolution_bitcast_fusion.3 = f32[2,5,3,14,14,14]{3,5,2,1,0,4:T(8,128)} fusion(f32[14,14,64,1,1,1]{2,1,5,4,3,0:T(8,128)S(1)} %copy-done.31, bf16[1,2,14,5,14,1,3,64]{7,6,4,3,5,2,1,0:T(4,128)(2,1)S(1)} %get-tuple-element.54), kind=kOutput, calls=%fused_computation.79 | convolution fusion | flops 63221760 | bytes 1132096 | tf_op jit(solution)/shard_map/gaibjhc,jlc->gabhijl/dot_general | solution.py:50
  143.3 12.1 convolution_bitcast_fusion.4
  155.4 22.0 %fusion.142 = (f32[2,5,3,14,14]{4,3,2,1,0:T(8,128)S(1)}, f32[2,5,3,14,14,14,14]{4,6,5,3,2,1,0:T(8,128)}) fusion(f32[2,5,3,14,14,14]{4,5,3,2,1,0:T(8,128)} %copy.109, bf16[1,2,14,5,14,1,3,64]{7,6,4,3,5,2,1,0:T(4,128)(2,1)S(1)} %copy-done.5, bf16[1,2,14,5,14,1,3,64]{7,6,4,3,5,2,1,0:T(4,128)(2,1)S(1)} %get-tuple-element.54, ...), kind=kOutput, calls=%fused_computation.219 | convolution fusion | flops 152121472 | bytes 6797280 | tf_op jit(solution)/shard_map/gaibjhc,gakblhc->gabhijkl/dot_general | solution.py:44
  177.4 20.1 %exponential_reduce_fusion = f32[2,5,3,14,14]{4,3,2,1,0:T(8,128)S(1)} fusion(f32[2,5,3,14,14,14,14]{4,6,5,3,2,1,0:T(8,128)} %get-tuple-element.61, f32[2,5,3,14,14]{4,3,2,1,0:T(8,128)S(1)} %get-tuple-element.60), kind=kLoop, calls=%fused_computation.5 | loop fusion | flops 2299080 | bytes 4656960 | tf_op jit(solution)/shard_map/reduce_sum | solution.py:147
  197.6 18.7 %fusion.55 = bf16[1,2,14,5,14,3,64]{6,4,2,5,3,1,0:T(8,128)(2,1)} fusion(f32[2]{0:T(128)S(1)} %add_convert_fusion.2, bf16[1,2,14,5,14,1,3,64]{7,6,4,3,5,2,1,0:T(4,128)(2,1)S(1)} %copy-done.6, f32[2,5,3,14,14,14,14]{4,6,5,3,2,1,0:T(8,128)} %get-tuple-element.61, f32[2,5,3,14,14]{4,3,2,1,0:T(8,128)S(1)} %log_add_fusion), kind=kOutput, calls=%fused_computation.98 | convolution fusion | flops 150575040 | bytes 6138728 | tf_op jit(solution)/shard_map/gabhijkl,gakblhc->gaibjhc/dot_general | solution.py:150
  236.7 40.7 %psum.92 = f32[]{:T(128)} all-reduce(f32[]{:T(128)} %convert_reduce_fusion.7), channel_id=1, replica_groups=mesh['img'=2,'tok'=4,'seq'=4] {'img','tok','seq'}, use_global_device_ids=true, to_apply=%region_9.10 | all-reduce | flops 1 | bytes 8 | tf_op jit(solution)/shard_map/psum | solution.py:190
  349.3 33.0 %multiply_reduce_fusion = (f32[2,5,3,14,14]{4,3,2,1,0:T(8,128)}, f32[2,5,3,14,14,14,14]{4,6,5,3,2,1,0:T(8,128)}) fusion(f32[2,5,3,14,14,14,14]{4,6,5,3,2,1,0:T(8,128)} %get-tuple-element.61, f32[2,5,3,14,14]{4,3,2,1,0:T(8,128)S(1)} %log_add_fusion, bf16[1,2,14,5,14,1,3,64]{7,6,4,3,5,2,1,0:T(4,128)(2,1)} %get-tuple-element.53, ...), kind=kOutput, calls=%fused_computation.3 | convolution fusion | flops 150968992 | bytes 10772160 | tf_op jit(solution)/shard_map/gaibjhc,gakblhc->gabhijkl/dot_general | solution.py:240
  382.3 19.5 %fusion.56 = bf16[1,2,14,5,14,3,64]{6,4,2,5,3,1,0:T(8,128)(2,1)} fusion(bf16[2,14,5,14,3,64,1]{5,4,3,2,1,0,6:T(4,128)(2,1)S(1)} %fusion.39, f32[2,5,3,14,14,14,14]{4,6,5,3,2,1,0:T(8,128)} %get-tuple-element.61, f32[2,5,3,14,14]{4,3,2,1,0:T(8,128)S(1)} %log_add_fusion), kind=kOutput, calls=%fused_computation.99 | convolution fusion | flops 150198720 | bytes 6138720 | tf_op jit(solution)/shard_map/gabhijkl,gaibjhc->gakblhc/dot_general | solution.py:237
  401.8 44.6 %convert_reduce_fusion = (f32[2,5,3,14,14,14]{4,5,3,2,1,0:T(8,128)S(1)}, f32[2,5,3,14,14,14]{4,5,3,2,1,0:T(8,128)S(1)}, bf16[2,5,3,14,14,14,14]{4,6,5,3,2,1,0:T(8,128)(2,1)}) fusion(f32[2,5,3,14,14,14,14]{4,6,5,3,2,1,0:T(8,128)} %get-tuple-element.68, f32[2,5,3,14,14]{4,3,2,1,0:T(8,128)S(1)} %copy-done.34, f32[2,5,3,14,14,14,14]{4,6,5,3,2,1,0:T(8,128)} %get-tuple-element.61, ...), kind=kLoop, calls=%fused_computation | loop fusion | flops 7902720 | bytes 12230400 | tf_op jit(solution)/shard_map/reduce_sum | solution.py:259
  459.1 8.5 fusion.144
  467.6 12.9 %fusion.61 = bf16[1,2,14,5,14,3,64]{6,4,2,5,3,1,0:T(8,128)(2,1)} fusion(bf16[2,5,3,14,14,14,14]{4,6,5,3,2,1,0:T(8,128)(2,1)} %get-tuple-element.48, bf16[1,2,14,5,14,1,3,64]{7,6,4,3,5,2,1,0:T(4,128)(2,1)S(1)} %copy-done.3), kind=kOutput, calls=%fused_computation.100 | convolution fusion | flops 148270080 | bytes 3810240 | tf_op jit(solution)/shard_map/gabhijkl,gaibjhc->gakblhc/dot_general | solution.py:252
  480.5 14.9 %fusion.22 = bf16[1,2,14,5,14,3,64]{6,4,2,5,3,1,0:T(8,128)(2,1)} fusion(f32[14,64,2,5,3,14]{1,5,0,4,3,2:T(8,128)} %fusion.120, f32[14,64,2,5,3,14]{1,5,4,3,2,0:T(8,128)} %fusion.144, bf16[2,5,3,14,14,14,14]{4,6,5,3,2,1,0:T(8,128)(2,1)} %get-tuple-element.48, bf16[1,2,14,5,14,1,3,64]{7,6,4,3,5,2,1,0:T(4,128)(2,1)} %get-tuple-element.55), kind=kOutput, calls=%fused_computation.40 | convolution fusion | flops 149022720 | bytes 6820800 | tf_op jit(solution)/shard_map/gabhijkl,gakblhc->gaibjhc/dot_general | solution.py:246
  536.2 9.5 copy.162
  545.7 10.7 reshape.694
  578.2 10.9 all-to-all-done.3
  605.0 8.1 reshape.685
  618.7 463.4 %all-reduce.10 = (f32[]{:T(128)}, f32[768]{0:T(1024)}, f32[768]{0:T(1024)}, bf16[1769472]{0:T(1024)(128)(2,1)}, f32[768]{0:T(1024)}, /*index=5*/f32[768]{0:T(102...) all-reduce(f32[]{:T(128)} %get-tuple-element.56, ...), channel_id=1, replica_groups=mesh['img'=2,'tok'=4,'seq'=4] {'img','tok','seq'}, use_global_device_ids=true, to_apply=%region_7.8 | all-reduce | flops 7090561 | bytes 42568712 | tf_op jit(solution)/shard_map/psum | solution.py:190
  1088.5 21.3 %all_gather.33 = bf16[294912]{0:T(1024)(128)(2,1)S(1)} all-gather(bf16[18432]{0:T(1024)(128)(2,1)S(1)} %dynamic-slice.15), channel_id=1, replica_groups=mesh['img'=2,'tok'=4,'seq'=4] {'tok','seq'}, dimensions={0}, use_global_device_ids=true | all-gather | bytes 626688 | tf_op jit(solution)/shard_map/all_gather | solution.py:325
  1113.4 10.7 all-gather.16.cloned.1.call-done
  1128.8 38.3 %all-gather.18.cloned.1.call-done = bf16[1179648]{0:T(1024)(128)(2,1)} async-done(((bf16[73728]{0:T(1024)(128)(2,1)}), bf16[1179648]{0:T(1024)(128)(2,1)}) %all-gather.18.cloned.1.call-update) | async-done | bytes 2359312 | tf_op jit(solution)/shard_map/all_gather | solution.py:328
  1172.0 39.0 %all-gather.20.cloned.1.call-done = bf16[1179648]{0:T(1024)(128)(2,1)} async-done(((bf16[73728]{0:T(1024)(128)(2,1)}), bf16[1179648]{0:T(1024)(128)(2,1)}) %all-gather.20.cloned.1.call-update) | async-done | bytes 2359312 | tf_op jit(solution)/shard_map/all_gather | solution.py:331
  (287 shorter events, 252.1 us)
Async XLA Ops:
  7.2 64.6 %copy-start = (f32[27,64]{1,0:T(8,128)S(1)}, f32[27,64]{1,0:T(8,128)}, u32[]{:S(2)}) copy-start(f32[27,64]{1,0:T(8,128)} %param.29) | copy-start | bytes 20740
  7.2 54.5 %all-gather.8.cloned.1.call-start = ((), (), s32[]{:S(2)}) async-start(), calls=%async_computation.4 | async-start | bytes 5308416 | tf_op jit(solution)/shard_map/all_gather | solution.py:102
  8.0 53.7 %copy-start.53 = (f32[768]{0:T(1024)S(1)}, f32[768]{0:T(1024)}, u32[]{:S(2)}) copy-start(f32[768]{0:T(1024)} %param.23) | copy-start | bytes 9220
  8.0 53.7 %copy-start.68 = (f32[768]{0:T(1024)S(1)}, f32[768]{0:T(1024)}, u32[]{:S(2)}) copy-start(f32[768]{0:T(1024)} %param.24) | copy-start | bytes 9220
  8.0 271.0 %all-gather.10.cloned.1.call-start = ((), (), s32[]{:S(2)}) async-start(), calls=%async_computation.5 | async-start | bytes 1769472 | tf_op jit(solution)/shard_map/all_gather | solution.py:103
  8.7 272.5 %all-gather.12.cloned.1.call-start = ((), (), s32[]{:S(2)}) async-start(), calls=%async_computation.6 | async-start | bytes 7077888 | tf_op jit(solution)/shard_map/all_gather | solution.py:104
  9.5 286.1 %all-gather.14.cloned.1.call-start = ((), (), s32[]{:S(2)}) async-start(), calls=%async_computation.7 | async-start | bytes 7077888 | tf_op jit(solution)/shard_map/all_gather | solution.py:105
  10.4 54.5 %copy-start.40 = (f32[4,64]{1,0:T(4,128)}, f32[4,64]{1,0:T(4,128)S(1)}, u32[]{:S(2)}) copy-start(f32[4,64]{1,0:T(4,128)S(1)} %broadcast_multiply_fusion.1) | copy-start | bytes 3076
  10.7 54.3 %copy-start.50 = (f32[4,64]{1,0:T(4,128)}, f32[4,64]{1,0:T(4,128)S(1)}, u32[]{:S(2)}) copy-start(f32[4,64]{1,0:T(4,128)S(1)} %fusion.104) | copy-start | bytes 3076
  10.7 54.2 %copy-start.43 = (f32[4,64]{1,0:T(4,128)}, f32[4,64]{1,0:T(4,128)S(1)}, u32[]{:S(2)}) copy-start(f32[4,64]{1,0:T(4,128)S(1)} %fusion.132) | copy-start | bytes 3076
  67.9 23.6 %all-to-all-start = ((bf16[1,4,64,3,4,192]{5,2,3,1,0,4:T(8,128)(2,1)}), bf16[1,4,64,3,4,192]{5,2,3,1,0,4:T(8,128)(2,1)S(1)}, u32[]{:S(2)}, u32[]{:S(2)}) async-start(bf16[1,4,64,3,4,192]{5,2,3,1,0,4:T(8,128)(2,1)} %copy.102), calls=%async_computation | async-start | bytes 3145728 | tf_op jit(solution)/shard_map/all_to_all | solution.py:115
  91.6 15.8 %collective-permute-start = (bf16[1,6,64,3,192]{4,2,3,1,0:T(8,128)(2,1)S(1)}, bf16[1,6,64,3,192]{4,2,3,1,0:T(8,128)(2,1)S(1)}, u32[]{:S(2)}, u32[]{:S(2)}) collective-permute-start(bf16[1,6,64,3,192]{4,2,3,1,0:T(8,128)(2,1)S(1)} %slice.68), channel_id=1, source_target_pairs={{0,4},{4,8},{8,12},{1,5},{5,9},{9,13},{2,6},{6,10},{10,14},{3,7},{... | collective-permute-start | bytes 1327112 | tf_op jit(solution)/shard_map/ppermute | solution.py:19
  197.6 184.7 %copy-start.14 = (f32[2,5,3,14,14]{4,3,2,1,0:T(8,128)}, f32[2,5,3,14,14]{4,3,2,1,0:T(8,128)S(1)}, u32[]{:S(2)}) copy-start(f32[2,5,3,14,14]{4,3,2,1,0:T(8,128)S(1)} %log_add_fusion) | copy-start | bytes 70564
  221.9 57.2 %copy-start.59 = (f32[768]{0:T(1024)S(1)}, f32[768]{0:T(1024)}, u32[]{:S(2)}) copy-start(f32[768]{0:T(1024)} %param.31) | copy-start | bytes 9220
  223.2 8.4 collective-permute-start.1
  232.5 45.6 %all-to-all-start.1 = ((bf16[1,16,64,192]{3,2,0,1:T(8,128)(2,1)}), bf16[1,16,64,192]{3,2,0,1:T(8,128)(2,1)S(1)}, u32[]{:S(2)}, u32[]{:S(2)}) async-start(bf16[1,16,64,192]{3,2,0,1:T(8,128)(2,1)} %slice_add_fusion.1), calls=%async_computation.1 | async-start | bytes 1048576 | tf_op jit(solution)/shard_map/all_to_all | solution.py:169
  314.0 11.2 all-to-all-start.2
  328.5 10.8 collective-permute-start.2
  529.7 32.1 %collective-permute-start.3 = (bf16[1,6,64,3,192]{4,2,3,1,0:T(8,128)(2,1)S(1)}, bf16[1,6,64,3,192]{4,2,3,1,0:T(8,128)(2,1)S(1)}, u32[]{:S(2)}, u32[]{:S(2)}) collective-permute-start(bf16[1,6,64,3,192]{4,2,3,1,0:T(8,128)(2,1)S(1)} %slice.76), channel_id=1, source_target_pairs={{4,0},{8,4},{12,8},{5,1},{9,5},{13,9},{6,2},{10,6},{14,10},{7,3},{... | collective-permute-start | bytes 1327112 | tf_op jit(solution)/shard_map/ppermute | solution.py:19
  564.5 24.5 %all-to-all-start.3 = ((bf16[1,16,64,3,1,192]{5,2,4,3,0,1:T(8,128)(2,1)}), bf16[1,16,64,3,1,192]{5,2,4,3,0,1:T(8,128)(2,1)}, u32[]{:S(2)}, u32[]{:S(2)}) async-start(bf16[1,16,64,3,1,192]{5,2,4,3,0,1:T(8,128)(2,1)} %fusion.54), calls=%async_computation.3 | async-start | bytes 3145728 | tf_op jit(solution)/shard_map/all_to_all | solution.py:288
  569.0 555.1 %all-gather.16.cloned.1.call-start = ((), (), s32[]{:S(2)}) async-start(), calls=%async_computation.8 | async-start | bytes 1880064 | tf_op jit(solution)/shard_map/all_gather | solution.py:322
  1083.8 83.3 %all-gather.18.cloned.1.call-start = ((), (), s32[]{:S(2)}) async-start(), calls=%async_computation.9 | async-start | bytes 2506752 | tf_op jit(solution)/shard_map/all_gather | solution.py:328
  1085.4 125.6 %all-gather.20.cloned.1.call-start = ((), (), s32[]{:S(2)}) async-start(), calls=%async_computation.10 | async-start | bytes 2506752 | tf_op jit(solution)/shard_map/all_gather | solution.py:331
  1167.1 49.4 %copy-start.1 = (f32[27,64]{1,0:T(8,128)S(1)}, f32[27,64]{1,0:T(8,128)}, u32[]{:S(2)}) copy-start(f32[27,64]{1,0:T(8,128)} %param.29) | copy-start | bytes 20740
  (64 other events, 860.6 us)
Sparse Core Ops, SparseCore 0:
  9.6 52.0 all-gather.7
  63.3 22.7 all-gather.9
  87.6 62.6 all-gather.11
  151.7 62.6 all-gather.13
  1083.9 40.1 all-gather.15
  1126.2 40.8 all-gather.17
  1170.0 40.9 all-gather.19
where the time goes:
time: 1240 us; the launch traced here: 1220 us
  blocking collectives  525 us (42%)
  matrix products  223 us (18%)
  waiting for transfers between devices  191 us (15%)
  local copies, waits for them, and re-layouts  146 us (12%)
  other arithmetic  95.4 us (8%)
  starting transfers between devices  25.5 us (2%)
  between operations  18.5 us (1%)
    psum x2, blocking collectives, local(): lax.psum((squares_here, count_here), ('img', 'tok', 'seq'))  504 us
    all_gather x1, waiting for transfers between devices, local(): lax.all_gather(qkv_weight, 'img', axis=0, tiled=True)  50.9 us
    reduce_sum x1, other arithmetic, local(): col_terms = jnp.sum(score_wide, axis=-2)  44.6 us
    all_gather x1, waiting for transfers between devices, local(): lax.all_gather(flat_sums[3].astype(jnp.bfloat16), ('tok', 'seq'), axis=0,...  39 us
    all_gather x1, waiting for transfers between devices, local(): lax.all_gather(flat_sums[2].astype(jnp.bfloat16), ('tok', 'seq'), axis=0,...  38.3 us
    dot_general x1, matrix products, local(): jnp.einsum('gaibjhc,gakblhc->gabhijkl', grad_slot, values, preferred_elem...  33 us
    unnamed x155, local copies, waits for them, and re-layouts  27.1 us
  transfers between devices with their start and end apart: 15, of which 9 were waited for; matrix products, arithmetic and copies ran while one was open for 17% of the time, Pallas kernels for 0%

commit v1 on v0

v1 whole, which is shorter than its diff:
```python
import functools

import jax
import jax.numpy as jnp
import numpy as np
from jax import lax
from jax.experimental import pallas as pl
from jax.experimental.pallas import tpu as pltpu
from jax.sharding import Mesh
from jax.sharding import PartitionSpec as P

HD = 64
WIN = 14
SLOT = 16
EDGE = 8
EPS = 1e-06
KEYS = 256
LANES = 128
FAR = 128.0
BF = jnp.bfloat16
F32 = jnp.float32
SEQ = ("yy", "core")
EVERY = ("img", "tok", "yy", "core")


def swapped(block, axis):
    size = lax.axis_size(axis)
    return lax.ppermute(block, axis, [(i, size - 1 - i) for i in range(size)])


def moved(block, axis, pairs):
    return lax.ppermute(block, axis, pairs)


def pick(pair_low, pair_high, flag):
    return jnp.where(flag == 0, pair_low, pair_high)


def tie(*values):
    return lax.optimization_barrier(values)


def layout_marks(band, place):
    first, last = band == 0, band == lax.axis_size("tok") - 1
    turned = (first & (place == 0)) | (last & (place > 0))
    corner = first & (place == 2)
    edge = turned | jnp.where(first, place == 1, place == 0)
    start = 8 - 2 * band
    real = jnp.where(edge, WIN * EDGE, jnp.where(corner, EDGE * EDGE, 0))
    return (
        start, jnp.where(corner, 0, start), turned.astype(jnp.int32), real, first.astype(jnp.int32),
        band, lax.axis_index("yy"), lax.axis_index("core"),
    )


def whole_spec(shape):
    return pl.BlockSpec(shape, lambda *_: (0,) * len(shape))


def column_picks(ways, cols):
    out = np.zeros((ways, SLOT + EDGE, cols), np.float32)
    for s in range(ways):
        for j in range(SLOT):
            out[s, j, WIN * s + j] = 1.0
        for j in range(EDGE):
            out[s, SLOT + j, WIN * ways + j] = 1.0
    return out


def turn_picks():
    out = np.zeros((WIN * EDGE, EDGE * (SLOT + EDGE)), np.float32)
    for i in range(WIN):
        for j in range(EDGE):
            out[i * EDGE + j, j * (SLOT + EDGE) + i] = 1.0
    return out


def pack_kernel(picks, block, out):
    ways, full = out.shape[0], SLOT + EDGE
    for r in range(block.shape[1]):
        both = jnp.dot(picks[...], block[0, r], preferred_element_type=F32)
        for s in range(ways):
            out[s, 0, r] = both[s * full : (s + 1) * full].astype(BF)


def packed(block):
    count, rows, cols, width = block.shape
    ways = lax.axis_size("yy") * lax.axis_size("core")
    full = SLOT + EDGE
    picks = jnp.asarray(column_picks(ways, cols).reshape(ways * full, cols), BF)
    return pl.pallas_call(
        pack_kernel,
        grid=(count,),
        in_specs=[
            whole_spec(picks.shape),
            pl.BlockSpec((1, rows, cols, width), lambda n: (n, 0, 0, 0)),
        ],
        out_specs=pl.BlockSpec((ways, 1, rows, full, width), lambda n: (0, n, 0, 0, 0)),
        out_shape=jax.ShapeDtypeStruct((ways, count, rows, full, width), BF),
        cost_estimate=pl.CostEstimate(flops=0, bytes_accessed=0, transcendentals=0),
        name="pack",
    )(picks, block)


def window_kernel(at, got, ring, turn, out):
    count, rows = got.shape[1], got.shape[2]
    start_a, start_e, turned, first = at[0], at[1], at[2], at[4]
    for n in range(count):

        def row_of(row, cols):
            own = jnp.maximum(row - 8, 0)
            before = ring[n, jnp.minimum(row, 7), cols].astype(F32)
            return jnp.where(row < 8, before, got[own // rows, n, own % rows, cols].astype(F32))

        for i in range(WIN):
            full = row_of(start_a + i, slice(0, SLOT))
            out[n, i * SLOT : (i + 1) * SLOT] = full.astype(BF)
        edge = jnp.concatenate(
            [row_of(start_e + i, slice(SLOT, SLOT + EDGE)) for i in range(WIN)], axis=0
        )
        tail = jnp.concatenate(
            [
                jnp.where(first == 1, ring[n, k], got[2 + k // rows, n, k % rows]).astype(F32)
                for k in range(EDGE)
            ],
            axis=0,
        ).astype(BF)
        bottom = jnp.dot(turn[...], tail, preferred_element_type=F32)
        out[n, WIN * SLOT :] = jnp.where(turned == 1, bottom, edge).astype(BF)


def window_norm_kernel(at, got, ring, turn, gain, shift, out, low):
    window_kernel(at, got, ring, turn, out)
    for start, size in ((0, WIN * SLOT), (WIN * SLOT, WIN * EDGE)):
        unit, _ = norm_parts(out[0, start : start + size].astype(F32))
        row = lax.broadcasted_iota(jnp.int32, (size, 1), 0)
        real = (row & (SLOT - 1)) < WIN if start == 0 else row < at[3]
        low[start : start + size] = jnp.where(real, unit * gain[...] + shift[...], 0.0).astype(BF)


def ring_rows(got, step):
    bands = lax.axis_size("tok")
    send = jnp.moveaxis(got[2:], 1, 0)
    send = send.reshape(send.shape[0], 8, SLOT + EDGE, send.shape[-1])
    return moved(send, "tok", [(i, (i + step) % bands) for i in range(bands)])


def windowed(got, ring, marks, norm=None):
    count, width = got.shape[1], got.shape[-1]
    tokens = WIN * (SLOT + EDGE)
    specs = [
        whole_spec(got.shape),
        whole_spec(ring.shape),
        whole_spec((WIN * EDGE, EDGE * (SLOT + EDGE))),
    ]
    out_specs = [whole_spec((count, tokens, width))]
    out_shape = [jax.ShapeDtypeStruct((count, tokens, width), BF)]
    if norm is not None:
        specs += [whole_spec((width,))] * 2
        out_specs.append(whole_spec((tokens, width)))
        out_shape.append(jax.ShapeDtypeStruct((tokens, width), BF))
    return pl.pallas_call(
        window_kernel if norm is None else window_norm_kernel,
        grid_spec=pltpu.PrefetchScalarGridSpec(
            num_scalar_prefetch=1, grid=(1,), in_specs=specs, out_specs=out_specs
        ),
        out_shape=out_shape,
        cost_estimate=pl.CostEstimate(flops=0, bytes_accessed=0, transcendentals=0),
        name="window",
    )(marks, got, ring, jnp.asarray(turn_picks(), BF), *(norm or ()))


def unwindow_kernel(at, *refs):
    flats, (turn, up, mid) = refs[:-3], refs[-3:]
    start_a, start_e, turned, first = at[0], at[1], at[2], at[4]
    full = SLOT + EDGE
    for n, flat in enumerate(flats):
        bottom = lax.dot_general(
            turn[...],
            flat[WIN * SLOT :].astype(BF),
            (((0,), (0,)), ((), ())),
            preferred_element_type=F32,
        )
        for row in range(24):
            i = row - start_e
            held = (i >= 0) & (i < WIN) & (turned == 0)
            at_row = pl.multiple_of(WIN * SLOT + EDGE * jnp.clip(i, 0, WIN - 1), EDGE)
            right = jnp.where(held, flat[pl.ds(at_row, EDGE)], 0.0)
            i = row - start_a
            at_row = pl.multiple_of(SLOT * jnp.clip(i, 0, WIN - 1), SLOT)
            left = jnp.where((i >= 0) & (i < WIN), flat[pl.ds(at_row, SLOT)], 0.0)
            if row < 8 or row >= 16:
                base = row % 8 * full
                here = (turned == 1) & (first == (1 if row < 8 else 0))
                left = jnp.where(here, bottom[base : base + SLOT], left)
            both = jnp.concatenate([left, right], axis=0).astype(BF)
            if row < 8:
                up[n, row] = both
            else:
                mid[n, row - 8] = both


def unwindowed(flats, marks):
    width = flats[0].shape[1]
    count, full = len(flats), SLOT + EDGE
    shapes = [(count, 8, full, width), (count, 16, full, width)]
    return pl.pallas_call(
        unwindow_kernel,
        grid_spec=pltpu.PrefetchScalarGridSpec(
            num_scalar_prefetch=1,
            grid=(1,),
            in_specs=[whole_spec(f.shape) for f in flats] + [whole_spec((WIN * EDGE, EDGE * full))],
            out_specs=[whole_spec(shape) for shape in shapes],
        ),
        out_shape=[jax.ShapeDtypeStruct(shape, BF) for shape in shapes],
        cost_estimate=pl.CostEstimate(flops=0, bytes_accessed=0, transcendentals=0),
        name="unwindow",
    )(marks, *flats, jnp.asarray(turn_picks(), BF))


def unpack_kernel(picks, got, *outs):
    for n, out in enumerate(outs):
        for r in range(got.shape[2]):
            total = None
            for s in range(got.shape[0]):
                part = lax.dot_general(
                    picks[s], got[s, n, r], (((0,), (0,)), ((), ())), preferred_element_type=F32
                )
                total = part if total is None else total + part
            out[r] = total.astype(out.dtype)


def unpacked(got, cols, dtypes):
    ways, count, rows, full, width = got.shape
    picks = column_picks(ways, cols)
    picks[:, WIN:SLOT] = 0.0
    return pl.pallas_call(
        unpack_kernel,
        in_specs=[whole_spec(picks.shape), whole_spec(got.shape)],
        out_specs=[whole_spec((rows, cols, width))] * count,
        grid=(1,),
        out_shape=[jax.ShapeDtypeStruct((rows, cols, width), dtype) for dtype in dtypes],
        cost_estimate=pl.CostEstimate(flops=0, bytes_accessed=0, transcendentals=0),
        name="unpack",
    )(jnp.asarray(picks, BF), got)


def exchanged(send):
    return lax.all_to_all(send, SEQ, split_axis=0, concat_axis=0, tiled=True)


def sent_back(up):
    bands = lax.axis_size("tok")
    return moved(up, "tok", [((i + 1) % bands, i) for i in range(bands)])


def band_rows_of(mid, ring):
    own = mid + jnp.pad(ring, ((0, 0), (8, 0), (0, 0), (0, 0)))
    ways = lax.axis_size("yy") * lax.axis_size("core")
    own = own.reshape(own.shape[0], ways, 16 // ways, SLOT + EDGE, own.shape[-1])
    return jnp.swapaxes(own, 0, 1)


def two_images():
    return lax.axis_size("img") == 2


def quarter(shard):
    if not two_images():
        return shard
    rows = shard.shape[0] // 4
    at = lax.axis_index("yy") * 2 + lax.axis_index("core")
    return lax.dynamic_slice_in_dim(shard, at * rows, rows, 0)


def half_of(shard, chunks=1):
    if not two_images():
        return [shard]
    rows = shard.shape[0] // (2 * chunks)
    first = lax.axis_index("core") * rows * chunks
    return [lax.dynamic_slice_in_dim(shard, first + i * rows, rows, 0) for i in range(chunks)]


def over_images(block):
    if two_images():
        return swapped(block, "img")
    return lax.all_gather(block, "img", axis=0, tiled=True)


def half_over_cores(block):
    return (block, swapped(block, "core")) if two_images() else block


def assembled_halves(shard, *parts):
    if not two_images():
        return parts[0]
    core, image = lax.axis_index("core"), lax.axis_index("img")
    other = jnp.concatenate(
        [pick(here, there, core) for here, there in parts]
        + [pick(there, here, core) for here, there in parts],
        axis=0,
    )
    return jnp.concatenate([pick(shard, other, image), pick(other, shard, image)], axis=0)


def gather_over_rows(block):
    return swapped(block, "yy") if two_images() else block


def gather_over_cores(first, second):
    if not two_images():
        return first
    high = lax.axis_index("yy")
    here = jnp.stack([pick(first, second, high), pick(second, first, high)])
    return here, swapped(here, "core")


def assembled(shard, parts):
    if not two_images():
        return parts
    here, there = parts
    core, image = lax.axis_index("core"), lax.axis_index("img")
    even, odd = pick(here, there, core), pick(there, here, core)
    other = jnp.stack([even, odd], axis=1).reshape(shard.shape)
    return jnp.concatenate([pick(shard, other, image), pick(other, shard, image)], axis=0)


def part_of(terms, dim, axis, other):
    index = lax.axis_index(axis)
    index = 1 - index if other else index
    return [lax.dynamic_index_in_dim(t, index, dim, keepdims=False) for t in terms]


def added(terms):
    total = terms[0].astype(F32)
    for t in terms[1:]:
        total = total + t.astype(F32)
    return total.astype(BF)


def to_send(terms, dim, axis):
    if lax.axis_size(axis) != 2:
        return jnp.moveaxis(added(terms), dim, 0)
    return added(part_of(terms, dim, axis, True))


def sent(block, axis):
    if lax.axis_size(axis) != 2:
        return lax.all_to_all(block, axis, split_axis=0, concat_axis=0, tiled=True)
    return swapped(block, axis)


def kept(terms, dim, axis, got):
    if lax.axis_size(axis) != 2:
        return [got[i] for i in range(got.shape[0])]
    return part_of(terms, dim, axis, False) + [got]


def split_grad(left, right):
    images, bands = lax.axis_size("img"), lax.axis_size("tok")
    core = lax.axis_index("core")
    rows, cols = left.shape[1], right.shape[1] // 2
    shape = (images, 2, bands, rows // images // 2 // bands, cols)

    def one(index):
        half = lax.dynamic_slice_in_dim(right, index * cols, cols, 1)
        return mm_tn(left, half).astype(BF).reshape(shape)

    return one(1 - core), one(core)


def crossed(block, distance):
    size = lax.axis_size("tok")
    return lax.ppermute(block, "tok", [(i, i ^ distance) for i in range(size)])


def band_parts(piece):
    band = lax.axis_index("tok")
    return [
        lax.dynamic_index_in_dim(piece, band ^ d, 0, keepdims=False)
        for d in range(lax.axis_size("tok"))
    ]


def over_bands(parts):
    return [crossed(part, d) for d, part in enumerate(parts) if d > 0]


def to_bands(total):
    return [crossed(total, d) for d in range(1, lax.axis_size("tok"))]


def final_kernel(splits, unit, at, near_own, near_other, far_own, far_other, *outs):
    band, core = at[5], at[7]

    def write(own, other):
        for t in range(own.shape[0]):
            to = t ^ band
            for (rows, first, blocks), out in zip(splits, outs):
                size = blocks * unit
                a = own[t, :, first * unit : first * unit + size].astype(F32)
                b = other[t, :, first * unit : first * unit + size].astype(F32)
                out[0, to, :, :size] = jnp.where(core == 0, a, b)
                out[0, to, :, size:] = jnp.where(core == 0, b, a)

    @pl.when(pl.program_id(0) == 0)
    def near():
        write(near_own, near_other)

    @pl.when(pl.program_id(0) == 1)
    def far():
        write(far_own, far_other)


def final(marks, own, other_core, beside, beside_other_core, splits):
    bands, rows, cols = own.shape
    unit = cols // sum(blocks for _, _, blocks in splits)
    outs = pl.pallas_call(
        functools.partial(final_kernel, splits, unit),
        grid_spec=pltpu.PrefetchScalarGridSpec(
            num_scalar_prefetch=1,
            grid=(2,),
            in_specs=[whole_spec(own.shape)] * 4,
            out_specs=[
                pl.BlockSpec((1, bands, n, 2 * blocks * unit), lambda y, at: (y ^ at[6], 0, 0, 0))
                for n, _, blocks in splits
            ],
        ),
        out_shape=[
            jax.ShapeDtypeStruct((2, bands, n, 2 * blocks * unit), F32) for n, _, blocks in splits
        ],
        cost_estimate=pl.CostEstimate(flops=0, bytes_accessed=0, transcendentals=0),
        name="final",
    )(marks, own, other_core, beside, beside_other_core)
    return [o.reshape(-1, o.shape[-1]) for o in outs]


def device_count():
    devices = 1
    for axis in EVERY:
        devices = devices * lax.axis_size(axis)
    return devices


def spread_sum(values):
    devices = device_count()
    part = -(-values.shape[0] // devices)
    cut = jnp.pad(values, (0, part * devices - values.shape[0])).reshape(devices, part)
    return jnp.sum(lax.all_to_all(cut, EVERY, split_axis=0, concat_axis=0, tiled=True), axis=0)


def all_counts(value):
    wide = jnp.broadcast_to(value, (device_count(), 8, LANES))
    got = lax.all_to_all(wide, EVERY, split_axis=0, concat_axis=0, tiled=True)
    return got


def to_all(part):
    wide = jnp.broadcast_to(part[None], (device_count(),) + part.shape)
    return lax.all_to_all(wide, EVERY, split_axis=0, concat_axis=0, tiled=True)


def rolled(block, amount):
    return pltpu.roll(block, amount, 1, stride=1, stride_axis=0)


def rel_places():
    size = 2 * WIN - 1
    out = np.zeros((4, LANES, size), np.float32)
    for m in range(size):
        out[0, size - 1 - m, m] = 1.0
        out[1, 32 + size - 1 - m, m] = 1.0
        out[2, m, m] = 1.0
        out[3, 64 + m, m] = 1.0
    return out


def head_places():
    out = np.zeros((2, HD, LANES), np.float32)
    for c in range(HD):
        out[0, c, c] = 1.0
        out[1, c, HD + c] = 1.0
    return out


def build_rel(tables, places, heads, out):
    for half in (0, 1):
        total = None
        for table, place in zip(tables, places):
            high = table.astype(BF)
            value = (table - high.astype(F32)).astype(BF) if half else high
            part = jnp.dot(place, value, preferred_element_type=F32)
            total = part if total is None else total + part
        for head in (0, 1):
            lanes = jnp.dot(total.astype(BF), heads[head], preferred_element_type=F32)
            out[head, :, half * LANES : (half + 1) * LANES] = lanes.astype(BF)


def build_both(at, rows, cols, places, heads, rel_a, rel_b):
    @pl.when(pl.program_id(0) == 0)
    def build():
        turned = at[2] == 1
        build_rel((rows[...], cols[...]), places, heads, rel_a)
        first = jnp.where(turned, cols[...], rows[...])
        second = jnp.where(turned, rows[...], cols[...])
        build_rel((first, second), places, heads, rel_b)


def wide_queries(q, rel, group):
    m = q.shape[0]
    terms = lax.dot_general(
        jnp.concatenate([q, q], axis=1), rel, (((1,), (1,)), ((), ())), preferred_element_type=F32
    )
    lane = lax.broadcasted_iota(jnp.int32, (group, LANES), 1)
    blocks = []
    for i in range(WIN):
        t = terms[i * group : (i + 1) * group]
        by_row = pltpu.roll(t, (LANES - (WIN - 1) + i) % LANES, 1)
        by_col = rolled(t, 19)
        blocks.append(jnp.where(lane < 64, by_row, by_col))
    both = jnp.concatenate(blocks, axis=0)
    high = both.astype(BF).astype(F32)
    low = pltpu.roll(both - high, 32, 1)
    lane = lax.broadcasted_iota(jnp.int32, (m, LANES), 1)
    mixed = jnp.where((lane & 63) < 32, high, low)
    mixed = jnp.where(lane == LANES - 1, 1.0, mixed)
    return jnp.concatenate([q * BF(HD**-0.5), mixed.astype(BF)], axis=1)


def full_keys(k, v, v_pad):
    n = k.shape[0]
    zeros = jnp.zeros((KEYS - n, LANES), BF)
    if v_pad is None:
        return jnp.concatenate([k, zeros], axis=0), jnp.concatenate([v, zeros], axis=0)
    fill = jnp.broadcast_to(v_pad, (KEYS - n, LANES)).astype(BF)
    return jnp.concatenate([k, zeros], axis=0), jnp.concatenate([v, fill], axis=0)


def only(block, head):
    lane = lax.broadcasted_iota(jnp.int32, block.shape, 1)
    return jnp.where((lane < HD) == (head == 0), block, jnp.zeros_like(block))


def attend(q, k, v, v_pad, rel_ref, hot, group, probs_ref):
    keys, vals = full_keys(k, v, v_pad)
    out = None
    for head in (0, 1):
        wide = wide_queries(q, rel_ref[head], group)
        scores = lax.dot_general(
            wide,
            jnp.concatenate([only(keys, head), hot], axis=1),
            (((1,), (1,)), ((), ())),
            preferred_element_type=F32,
        )
        top = jnp.max(scores, axis=1, keepdims=True)
        e = jnp.exp(scores - top)
        total = jnp.sum(e, axis=1, keepdims=True)
        p = (e * (1.0 / total)).astype(BF)
        probs_ref[head] = p
        part = jnp.dot(p, only(vals, head), preferred_element_type=F32)
        out = part if out is None else out + part
    return out.astype(BF)


def attend_kernel(
    at, q, k, v, v_pad, rows, cols, places, heads, hot_a, hot_b, out, probs_a, probs_b, rel_a, rel_b
):
    build_both(at, rows, cols, (places[0], places[1]), heads, rel_a, rel_b)
    n = WIN * SLOT
    pad = v_pad[...].astype(BF)
    out[:n] = attend(q[:n], k[:n], v[:n], None, rel_a, hot_a[...], SLOT, probs_a)
    out[n:] = attend(q[n:], k[n:], v[n:], pad, rel_b, hot_b[...], EDGE, probs_b)


def attend_back(q, k, v, v_pad, out_grad, rel_ref, hot, group, probs_ref, rel_grad):
    keys, vals = full_keys(k, v, v_pad)
    scale = HD**-0.5
    lane = lax.broadcasted_iota(jnp.int32, (group, LANES), 1)
    pair = lax.broadcasted_iota(jnp.int32, (KEYS, LANES), 1)
    dq, dks, dvs = None, [], []
    for head in (0, 1):
        probs = probs_ref[head]
        wide = probs.astype(F32)
        dp = lax.dot_general(
            out_grad, only(vals, head), (((1,), (1,)), ((), ())), preferred_element_type=F32
        )
        inner = jnp.sum(wide * dp, axis=1, keepdims=True)
        ds = (wide * (dp - inner)).astype(BF)
        both = jnp.dot(
            ds, jnp.concatenate([only(keys, head), hot], axis=1), preferred_element_type=F32
        )
        part = both[:, :LANES] * scale
        blocks = []
        for i in range(WIN):
            t = both[i * group : (i + 1) * group, LANES:]
            by_row = pltpu.roll(jnp.where(lane < WIN, t, 0.0), i, 1) if i else jnp.where(
                lane < WIN, t, 0.0
            )
            by_col = rolled(jnp.where((lane >= 64) & (lane < 64 + WIN), t, 0.0), 0)
            blocks.append(by_row + by_col)
        terms = jnp.concatenate(blocks, axis=0)
        high = terms.astype(BF)
        low = (terms - high.astype(F32)).astype(BF)
        split = jnp.concatenate([high, low], axis=1)
        rel = rel_ref[head]
        part = part + jnp.dot(
            split,
            jnp.concatenate([rel[:, :LANES], rel[:, :LANES]], axis=0),
            preferred_element_type=F32,
        )
        part = part + jnp.dot(high, rel[:, LANES:], preferred_element_type=F32)
        dq = part if dq is None else dq + part
        rel_grad[head] += lax.dot_general(
            split, q, (((0,), (0,)), ((), ())), preferred_element_type=F32
        )
        dks.append(
            lax.dot_general(ds, q, (((0,), (0,)), ((), ())), preferred_element_type=F32) * scale
        )
        dvs.append(
            lax.dot_general(probs, out_grad, (((0,), (0,)), ((), ())), preferred_element_type=F32)
        )
    dk = jnp.where(pair < HD, dks[0], dks[1]).astype(BF)
    dv = jnp.where(pair < HD, dvs[0], dvs[1]).astype(BF)
    return dq.astype(BF), dk, dv


def attend_back_kernel(
    at, q, k, v, v_pad, rows, cols, places, heads, hot_a, hot_b, grad, probs_a, probs_b,
    dqkv, pad_sum, rows_grad, cols_grad, rel_a, rel_b, acc_a, acc_b,
):
    step = pl.program_id(0)
    steps = dqkv.shape[1] // (3 * LANES)
    build_both(at, rows, cols, (places[2], places[3]), heads, rel_a, rel_b)

    @pl.when(step == 0)
    def clear():
        acc_a[...] = jnp.zeros_like(acc_a)
        acc_b[...] = jnp.zeros_like(acc_b)

    n = WIN * SLOT
    pad = v_pad[...].astype(BF)
    part_a = attend_back(
        q[:n], k[:n], v[:n], None, grad[:n], rel_a, hot_a[...], SLOT, probs_a, acc_a
    )
    part_b = attend_back(
        q[n:], k[n:], v[n:], pad, grad[n:], rel_b, hot_b[...], EDGE, probs_b, acc_b
    )
    for i in range(3):
        to = pl.ds(pl.multiple_of((i * steps + step) * LANES, LANES), LANES)
        dqkv[:n, to] = part_a[i][:n]
        dqkv[n:, to] = part_b[i][: WIN * EDGE]
    pad_sum[...] = jnp.sum(part_b[2][WIN * EDGE :].astype(F32), axis=0, keepdims=True)

    @pl.when(step == steps - 1)
    def tables():
        def table(acc):
            even = acc[0, :LANES] + acc[0, LANES:]
            odd = acc[1, :LANES] + acc[1, LANES:]
            return even + pltpu.roll(odd, HD, 1)

        size = 2 * WIN - 1
        a, b = table(acc_a), table(acc_b)
        turned = at[2] == 1
        low, high = slice(0, size), slice(64, 64 + size)
        rows_grad[...] = a[low, :HD] + jnp.where(turned, b[high, :HD], b[low, :HD])
        cols_grad[...] = a[high, :HD] + jnp.where(turned, b[low, :HD], b[high, :HD])


def hot_tables():
    def table(place):
        out = np.zeros((2, KEYS, LANES), np.float32)
        for key in range(KEYS):
            at = place(key)
            if at is None:
                out[0, key, LANES - 1] = -1e30
            else:
                for base, index in ((0, at[0]), (32, at[0]), (64, at[1]), (96, at[1])):
                    out[0, key, base + index] = 1.0
                out[1, key, WIN - 1 - at[0]] = 1.0
                out[1, key, 64 + WIN - 1 - at[1]] = 1.0
        return out

    def whole(key):
        i, j = divmod(key, SLOT)
        return (i, j) if i < WIN and j < WIN else None

    def partial(key):
        if key < WIN * EDGE:
            return divmod(key, EDGE)
        i, j = divmod(key - WIN * EDGE, EDGE)
        return (i, EDGE + j) if i < WIN and EDGE + j < WIN else None

    return table(whole), table(partial)


def attention(qkv, v_pad, rel_rows, rel_cols, marks):
    tokens_a, tokens_b = WIN * SLOT, WIN * EDGE
    tokens, width = qkv.shape[0], qkv.shape[1] // 3
    pairs = width // LANES
    table = (2 * WIN - 1, HD)
    hots = [jnp.asarray(t, BF) for t in hot_tables()]
    places, heads = jnp.asarray(rel_places(), BF), jnp.asarray(head_places(), BF)

    def cols(n, base):
        return pl.BlockSpec((n, LANES), lambda p, at: (0, base * pairs + p))

    specs = [cols(tokens, i) for i in range(3)] + [
        pl.BlockSpec((LANES,), lambda p, at: (p,)),
        whole_spec(table),
        whole_spec(table),
        whole_spec(places.shape),
        whole_spec(heads.shape),
        whole_spec((KEYS, LANES)),
        whole_spec((KEYS, LANES)),
    ]
    probs_specs = [
        pl.BlockSpec((2, tokens_a, KEYS), lambda p, at: (p, 0, 0)),
        pl.BlockSpec((2, tokens_b, KEYS), lambda p, at: (p, 0, 0)),
    ]
    rel_scratch = [pltpu.VMEM((2, LANES, 2 * LANES), BF)] * 2
    shared = (marks, qkv, qkv, qkv, v_pad, rel_rows, rel_cols, places, heads)
    out, probs_a, probs_b = pl.pallas_call(
        attend_kernel,
        grid_spec=pltpu.PrefetchScalarGridSpec(
            num_scalar_prefetch=1,
            grid=(pairs,),
            in_specs=specs,
            out_specs=[cols(tokens, 0)] + probs_specs,
            scratch_shapes=rel_scratch,
        ),
        out_shape=[
            jax.ShapeDtypeStruct((tokens, width), BF),
            jax.ShapeDtypeStruct((2 * pairs, tokens_a, KEYS), BF),
            jax.ShapeDtypeStruct((2 * pairs, tokens_b, KEYS), BF),
        ],
        cost_estimate=pl.CostEstimate(flops=0, bytes_accessed=0, transcendentals=0),
        name="attend",
    )(*shared, hots[0][0], hots[1][0])

    def back(grad):
        return pl.pallas_call(
            attend_back_kernel,
            grid_spec=pltpu.PrefetchScalarGridSpec(
                num_scalar_prefetch=1,
                grid=(pairs,),
                in_specs=specs + [cols(tokens, 0)] + probs_specs,
                out_specs=[
                    whole_spec((tokens, 3 * width)),
                    cols(1, 0),
                    whole_spec(table),
                    whole_spec(table),
                ],
                scratch_shapes=rel_scratch + [pltpu.VMEM((2, 2 * LANES, LANES), F32)] * 2,
            ),
            out_shape=[
                jax.ShapeDtypeStruct((tokens, 3 * width), BF),
                jax.ShapeDtypeStruct((1, width), F32),
                jax.ShapeDtypeStruct(table, F32),
                jax.ShapeDtypeStruct(table, F32),
            ],
            cost_estimate=pl.CostEstimate(flops=0, bytes_accessed=0, transcendentals=0),
            name="attend_back",
        )(*shared, hots[0][1], hots[1][1], grad, probs_a, probs_b)

    return out, back


def norm_parts(values):
    centre = jnp.mean(values, axis=-1, keepdims=True)
    centred = values - centre
    spread = jnp.mean(centred * centred, axis=-1, keepdims=True)
    scale = lax.rsqrt(spread + EPS)
    return centred * scale, scale


def norm_back(grad, unit, scale, gain):
    g = grad * gain
    mean = jnp.mean(g, axis=-1, keepdims=True)
    along = jnp.mean(g * unit, axis=-1, keepdims=True)
    return scale * (g - mean - unit * along)


def mm(a, b):
    return jnp.dot(a, b, preferred_element_type=F32)


def mm_nt(a, b):
    return lax.dot_general(a, b, (((1,), (1,)), ((), ())), preferred_element_type=F32)


def mm_tn(a, b):
    return lax.dot_general(a, b, (((0,), (0,)), ((), ())), preferred_element_type=F32)


def local(
    images, teacher, valid_mask, out_grad, attn_gain, attn_shift, qkv_weight, query_bias,
    value_bias, rel_rows, rel_cols, proj_weight, proj_bias, mlp_gain, mlp_shift, up_weight,
    up_bias, down_weight, down_bias,
):
    band = lax.axis_index("tok")
    bands = lax.axis_size("tok")
    place = lax.axis_index("yy") * lax.axis_size("core") + lax.axis_index("core")
    width = images.shape[-1]
    image_rows = images.shape[1] * bands * lax.axis_size("yy") * lax.axis_size("core")
    tokens_all = images.shape[0] * lax.axis_size("img") * image_rows * images.shape[2]

    marks = layout_marks(band, place)
    real_edge = marks[3]
    marks = jnp.stack(marks).astype(jnp.int32)
    x_got = exchanged(packed(images))
    qkv_1 = over_images(quarter(qkv_weight))
    proj_1 = [over_images(c) for c in half_of(proj_weight)]
    up_1 = [over_images(c) for c in half_of(up_weight, 2)]
    down_1 = [over_images(c) for c in half_of(down_weight, 2)]
    x_got, qkv_1, marks = tie(x_got, qkv_1, marks)
    qkv_2 = gather_over_rows(qkv_1)
    x_ring = ring_rows(x_got, 1)
    marked = jnp.where(valid_mask[..., None] > 0, teacher, jnp.full_like(teacher, FAR))
    late_pack = packed(tie(jnp.concatenate([marked, out_grad], axis=0), qkv_1)[0])
    qkv_2, x_ring, x_got, late_pack, up_1[0] = tie(qkv_2, x_ring, x_got, late_pack, up_1[0])
    qkv_3 = gather_over_cores(qkv_1, qkv_2)
    x_low, tokens_low = windowed(x_got, x_ring, marks, (attn_gain, attn_shift))
    x_low = x_low[0]
    qkv_3, x_low, tokens_low, proj_1[0] = tie(qkv_3, x_low, tokens_low, proj_1[0])
    proj_2 = half_over_cores(proj_1[0])

    row_a = lax.broadcasted_iota(jnp.int32, (WIN * SLOT, 1), 0)
    row_b = lax.broadcasted_iota(jnp.int32, (WIN * EDGE, 1), 0)
    real = jnp.concatenate(
        [(row_a & (SLOT - 1)) < WIN, row_b < real_edge], axis=0
    )
    inputs = x_low.astype(F32)
    qkv_bias = jnp.concatenate([query_bias, jnp.zeros_like(query_bias), value_bias])
    qkv_full = assembled(qkv_weight, qkv_3)
    qkv = (mm(tokens_low, qkv_full) + qkv_bias).astype(BF)
    qkv, late_pack, proj_2, up_1 = tie(qkv, late_pack, proj_2, up_1)
    up_2 = [half_over_cores(c) for c in up_1]
    late_got = exchanged(late_pack)
    attended, attention_back = attention(qkv, value_bias, rel_rows, rel_cols, marks)
    proj_full = assembled_halves(proj_weight, proj_2)
    attended, up_2, proj_full, down_1[0] = tie(attended, up_2, proj_full, down_1[0])
    resid = inputs + mm(attended, proj_full) + proj_bias
    unit2, scale2 = norm_parts(resid)
    normed2 = (unit2 * mlp_gain + mlp_shift).astype(BF)
    up_full = assembled_halves(up_weight, *up_2)
    normed2, up_full, late_got = tie(normed2, up_full, late_got)
    late_ring = ring_rows(late_got, 1)
    counts = all_counts(jnp.sum(tie(valid_mask, late_got)[0].astype(F32)))
    hidden_pre = mm(normed2, up_full) + up_bias
    cdf = 0.5 * (1.0 + lax.erf(hidden_pre * (0.5**0.5)))
    hidden = (hidden_pre * cdf).astype(BF)
    slope = cdf + hidden_pre * jnp.exp(-0.5 * hidden_pre * hidden_pre) * ((2 * np.pi) ** -0.5)
    hidden, slope, late_ring, down_1, counts = tie(hidden, slope, late_ring, down_1, counts)
    count_total = jnp.sum(counts[:, 0, 0])
    down_2 = [half_over_cores(c) for c in down_1]
    (late,) = windowed(late_got, late_ring, marks)
    late, down_2 = tie(late, down_2)
    down_full = assembled_halves(down_weight, *down_2)
    result = resid + mm(hidden, down_full) + down_bias

    teach = late[0].astype(F32)
    valid = (real & (teach[:, :1] < 0.5 * FAR)).astype(F32)
    differ = valid * (result - teach)
    squares = jnp.sum(differ * differ)
    grads = jnp.where(real, late[1], jnp.zeros_like(late[1])).astype(F32)
    result_grad = grads + differ * (tokens_all / (4.0 * count_total))
    down_in = result_grad.astype(BF)

    d_send, d_keep = split_grad(hidden, down_in)
    d_send, down_in = tie(d_send, down_in)
    d_got = sent(d_send, "core")
    pre_grad = (slope * mm_nt(down_in, down_full)).astype(BF)
    d_got, d_keep, pre_grad = tie(d_got, d_keep, pre_grad)
    d_terms = [d_keep, d_got]
    d_out, pre_grad = tie(to_send(d_terms, 0, "img"), pre_grad)
    d_got = sent(d_out, "img")
    u_send, u_keep = split_grad(normed2, pre_grad)
    u_send, pre_grad = tie(u_send, pre_grad)
    u_got = sent(u_send, "core")
    normed2_grad = mm_nt(pre_grad, up_full)
    u_got, u_keep, normed2_grad = tie(u_got, u_keep, normed2_grad)
    u_terms = [u_keep, u_got]
    u_out, normed2_grad = tie(to_send(u_terms, 1, "yy"), normed2_grad)
    u_got = sent(u_out, "yy")
    resid_grad = result_grad + norm_back(normed2_grad, unit2, scale2, mlp_gain)
    proj_in = resid_grad.astype(BF)
    p_send, p_keep = split_grad(attended, proj_in)
    p_send, proj_in = tie(p_send, proj_in)
    p_got = sent(p_send, "core")
    attended_grad = mm_nt(proj_in, proj_full).astype(BF)
    attended_grad, p_got, p_keep = tie(attended_grad, p_got, p_keep)
    p_terms = [p_keep, p_got]
    p_out, attended_grad = tie(to_send(p_terms, 0, "img"), attended_grad)
    p_got = sent(p_out, "img")

    dqkv, pad_sum, rel_rows_grad, rel_cols_grad = attention_back(attended_grad)
    dqkv, pad_sum, d_got, u_got = tie(dqkv, pad_sum, d_got, u_got)
    d_terms = kept(d_terms, 0, "img", d_got)
    u_terms = kept(u_terms, 1, "yy", u_got)
    d_out, u_out, dqkv = tie(to_send(d_terms, 0, "yy"), to_send(u_terms, 0, "img"), dqkv)
    d_got = sent(d_out, "yy")
    u_got = sent(u_out, "img")
    q_send, q_keep = split_grad(tokens_low, dqkv)
    q_send, dqkv = tie(q_send, dqkv)
    q_got = sent(q_send, "core")
    normed_grad = jnp.where(real, mm_nt(dqkv, qkv_full), 0.0)
    normed_grad, q_got, q_keep, p_got = tie(normed_grad, q_got, q_keep, p_got)
    p_terms = kept(p_terms, 0, "img", p_got)
    half = bands // 2
    qa_terms = [q_keep[:, :, :half], q_got[:, :, :half]]
    qb_terms = [q_keep[:, :, half:], q_got[:, :, half:]]
    qa_out, qb_out, p_out, normed_grad = tie(
        to_send(qa_terms, 0, "img"), to_send(qb_terms, 1, "yy"), to_send(p_terms, 0, "yy"), normed_grad
    )
    qa_got = sent(qa_out, "img")
    qb_got = sent(qb_out, "yy")
    p_got = sent(p_out, "yy")
    unit, scale = norm_parts(inputs)
    images_grad = resid_grad + norm_back(normed_grad, unit, scale, attn_gain)
    down_bias_grad = jnp.sum(down_in.astype(F32), axis=0)
    up_bias_grad = jnp.sum(pre_grad.astype(F32), axis=0)
    mlp_gain_grad = jnp.sum(normed2_grad * unit2, axis=0)
    mlp_shift_grad = jnp.sum(normed2_grad, axis=0)
    proj_bias_grad = jnp.sum(proj_in.astype(F32), axis=0)
    qkv_sums = jnp.sum(dqkv.astype(F32), axis=0)
    query_bias_grad = qkv_sums[:width]
    value_bias_grad = qkv_sums[2 * width :] + pad_sum[0]
    attn_gain_grad = jnp.sum(normed_grad * unit, axis=0)
    attn_shift_grad = jnp.sum(normed_grad, axis=0)
    small = (
        squares.reshape(1), attn_gain_grad, attn_shift_grad, query_bias_grad, value_bias_grad,
        rel_rows_grad, rel_cols_grad, proj_bias_grad, mlp_gain_grad, mlp_shift_grad,
        up_bias_grad, down_bias_grad,
    )
    flat, images_grad = tie(jnp.concatenate([s.reshape(-1) for s in small]), images_grad)
    total = spread_sum(flat)
    backs = unwindowed([jnp.where(real, result, 0.0), images_grad], marks)
    backs, d_got, total = tie(backs, d_got, total)
    back_ring = sent_back(backs[0])
    d_parts = tie(*band_parts(added(kept(d_terms, 0, "yy", d_got))))
    d_got = over_bands(d_parts)
    u_got, p_got, d_parts = tie(u_got, p_got, d_parts)
    u_sum = added(kept(u_terms, 0, "img", u_got))
    p_sum = added(kept(p_terms, 0, "yy", p_got))
    part, cols = p_sum.shape[1], p_sum.shape[2]
    blocks = u_sum.shape[-1] // cols
    u_parts = tie(*band_parts(jnp.concatenate([u_sum, p_sum], axis=-1)))
    u_got = over_bands(u_parts)
    qa_got, qb_got, u_parts = tie(qa_got, qb_got, u_parts)
    qa_terms = kept(qa_terms, 0, "img", qa_got)
    qb_terms = kept(qb_terms, 1, "yy", qb_got)
    qa_out, qb_out = tie(to_send(qa_terms, 0, "yy"), to_send(qb_terms, 0, "img"))
    qa_got = sent(qa_out, "yy")
    qb_got = sent(qb_out, "img")
    back_ring, qa_out = tie(back_ring, qa_out)
    own_rows = band_rows_of(backs[1], back_ring)
    back_got = exchanged(own_rows)
    d_got, own_rows = tie(d_got, own_rows)
    d_sum = added([d_parts[0]] + d_got)
    d_all = to_bands(d_sum)
    qa_got, qb_got, d_sum = tie(qa_got, qb_got, d_sum)
    q_parts = tie(
        *band_parts(
            jnp.concatenate(
                [added(kept(qa_terms, 0, "yy", qa_got)), added(kept(qb_terms, 0, "img", qb_got))],
                axis=0,
            )
        )
    )
    q_got = over_bands(q_parts)
    u_got, q_parts, back_got = tie(u_got, q_parts, back_got)
    u_sum = added([u_parts[0]] + u_got)
    u_all = to_bands(u_sum)
    block_out, images_grad = unpacked(back_got, images.shape[2], (BF, F32))
    d_all, u_sum, block_out, total = tie(d_all, u_sum, block_out, total)
    d_own = jnp.stack([d_sum] + d_all)
    d_beside, d_other = swapped(d_own, "yy"), swapped(d_own, "core")
    q_got, d_own = tie(q_got, d_own)
    q_sum = added([q_parts[0]] + q_got)
    q_all = to_bands(q_sum)
    total = to_all(tie(total, q_sum)[0])
    d_beside, d_other, u_all, q_sum = tie(d_beside, d_other, u_all, q_sum)
    u_own = jnp.stack([u_sum] + u_all)
    u_beside, u_other = swapped(u_own, "yy"), swapped(u_own, "core")
    d_last = swapped(d_beside, "core")
    u_own, d_last, total = tie(u_own, d_last, total)
    (down_grad,) = final(marks, d_own, d_other, d_beside, d_last, ((d_own.shape[1], 0, 1),))
    q_all, down_grad = tie(q_all, down_grad)
    q_own = jnp.stack([q_sum] + q_all)
    q_beside, q_other = swapped(q_own, "yy"), swapped(q_own, "core")
    u_beside, q_own = tie(u_beside, q_own)
    u_last = swapped(u_beside, "core")
    up_grad, proj_grad = final(
        marks, u_own, u_other, u_beside, u_last, ((part, 0, blocks), (part, blocks, 1))
    )
    q_beside, up_grad = tie(q_beside, up_grad)
    q_last = swapped(q_beside, "core")
    (qkv_grad,) = final(marks, q_own, q_other, q_beside, q_last, ((q_own.shape[1], 0, 1),))
    total = total.reshape(-1)
    cut, at = [], 0
    for s in small:
        cut.append(total[at : at + s.size].reshape(s.shape))
        at += s.size
    distill_loss = cut[0][0] / (count_total * width)
    return (
        block_out[None], distill_loss, images_grad[None], cut[1], cut[2], qkv_grad, cut[3], cut[4],
        cut[5], cut[6], proj_grad, cut[7], cut[8], cut[9], up_grad, cut[10], down_grad, cut[11],
    )


def solution(mesh):
    shape = dict(mesh.shape)
    fine = Mesh(
        mesh.devices.reshape(shape["img"], shape["tok"], shape["seq"] // 2, 2), EVERY
    )
    tokens = P("img", ("tok",) + SEQ, None, None)
    mask = P("img", ("tok",) + SEQ, None)
    split, whole = P("img", None), P()
    return jax.shard_map(
        local,
        mesh=fine,
        in_specs=(
            tokens, tokens, mask, tokens, whole, whole, split, whole, whole, whole, whole, split,
            whole, whole, whole, split, whole, split, whole,
        ),
        out_specs=(
            tokens, whole, tokens, whole, whole, split, whole, whole, whole, whole, split, whole,
            whole, whole, split, whole, split, whole,
        ),
        check_vma=False,
    )
```

time: 1240 us -> 383 us (0.31)
  blocking collectives: 525 us -> 11.3 us
  matrix products: 223 us -> 41.3 us
  waiting for transfers between devices: 191 us -> 68.5 us
  local copies, waits for them, and re-layouts: 146 us -> 31.5 us
  Pallas kernels: 0 us -> 63.8 us
  starting transfers between devices: 25.5 us -> 80.2 us
  other arithmetic: 95.4 us -> 75.4 us
  between operations: 18.5 us -> 5.11 us
    psum x2 -> x0, blocking collectives: 504 us -> none  [local(): lax.psum((squares_here, count_here), ('img', 'tok', 'seq'))]
    dot_general x28 -> x16, matrix products: 223 us -> 41.3 us  [the longest x8 16.5 us: mm_tn(): lax.dot_general(a, b, (((0,), (0,)), ((), ())), preferred_element_type=F32)]
    all_gather x7 -> x0, waiting for transfers between devices: 139 us -> none  [the longest x1 50.9 us: local(): lax.all_gather(qkv_weight, 'img', axis=0, tiled=True)]
    pallas_call x0 -> x11, Pallas kernels: none -> 63.8 us  [the longest x1 18.3 us: back(): pl.pallas_call(attend_back_kernel, grid_spec=pltpu.PrefetchScalarGridSpec...]
    reduce_sum x13 -> x12, other arithmetic: 72.8 us -> 18.1 us  [the longest x1 9.73 us: local(): mlp_gain_grad = jnp.sum(normed2_grad * unit2, axis=0)]
    ppermute x4 -> x57, starting transfers between devices: 9.73 us -> 61.5 us  [the longest x18 30.6 us: crossed(): return lax.ppermute(block, 'tok', [(i, i ^ distance) for i in range(size)])]
    reshape x11 -> x6, local copies, waits for them, and re-layouts: 50.8 us -> 4.76 us  [the longest x2 1.36 us: local(): cut.append(total[at:at + s.size].reshape(s.shape))]
    ppermute x4 -> x57, waiting for transfers between devices: 18.5 us -> 57.3 us  [the longest x36 27.8 us: swapped(): return lax.ppermute(block, axis, [(i, size - 1 - i) for i in range(size)])]
  transfers between devices with their start and end apart: 15 -> 62, of which waited for: 9 -> 16; matrix products, arithmetic and copies ran while one was open for 17% -> 29% of each run, Pallas kernels for 0% -> 16%
where the time goes in v1:
time: 383 us; the launch traced here: 377 us
  starting transfers between devices  80.2 us (21%)
  other arithmetic  75.4 us (20%)
  waiting for transfers between devices  68.5 us (18%)
  Pallas kernels  63.8 us (17%)
  matrix products  41.3 us (11%)
  local copies, waits for them, and re-layouts  31.5 us (8%)
  blocking collectives  11.3 us (3%)
  between operations  5.11 us (1%)
    ppermute x18, starting transfers between devices, crossed(): return lax.ppermute(block, 'tok', [(i, i ^ distance) for i in range(size)])  30.6 us
    ppermute x36, waiting for transfers between devices, swapped(): return lax.ppermute(block, axis, [(i, size - 1 - i) for i in range(size)])  27.8 us
    convert_element_type x18, other arithmetic, added(): return total.astype(BF)  27.8 us
    ppermute x36, starting transfers between devices, swapped(): return lax.ppermute(block, axis, [(i, size - 1 - i) for i in range(size)])  24.3 us
    ppermute x18, waiting for transfers between devices, crossed(): return lax.ppermute(block, 'tok', [(i, i ^ distance) for i in range(size)])  22.8 us
    pallas_call x1, Pallas kernels, back(): pl.pallas_call(attend_back_kernel, grid_spec=pltpu.PrefetchScalarGridSpec...  18.3 us
    dot_general x8, matrix products, mm_tn(): lax.dot_general(a, b, (((0,), (0,)), ((), ())), preferred_element_type=F32)  16.5 us
    pallas_call x3, Pallas kernels, final(): pl.pallas_call(functools.partial(final_kernel, splits, unit), grid_spec=p...  14.1 us
  transfers between devices with their start and end apart: 62, of which 16 were waited for; matrix products, arithmetic and copies ran while one was open for 29% of the time, Pallas kernels for 16%

profile of v1, /device:TPU:0, one launch (start us, length us, event | category | flops | bytes accessed | tf_op | source)
XLA Modules:
  0.0 377.1 jit_solution(6365204428276091759)
XLA Ops:
  15.5 4.5 %all-to-all-done.got = bf16[4,1,4,24,768]{4,3,2,1,0:T(8,128)(2,1)S(1)} async-done(((bf16[4,1,4,24,768]{4,3,2,1,0:T(8,128)(2,1)}), bf16[4,1,4,24,768]{4,3,2,1,0:T(8,128)(2,1)S(1)}, u32[]{:S(2)}, u32[]{:S(2)}) %all-to-all-start) | async-done | bytes 589856 | tf_op jit(solution)/shard_map/all_to_all | solution.py:249
  28.2 3.7 collective-permute-done.2.ring
  51.9 5.9 %collective-permute-done.7 = bf16[96,3072]{1,0:T(8,128)(2,1)} collective-permute-done((bf16[96,3072]{1,0:T(8,128)(2,1)}, bf16[96,3072]{1,0:T(8,128)(2,1)}, u32[]{:S(2)}, u32[]{:S(2)}) %collective-permute-start.7) | collective-permute-done | bytes 589856 | tf_op jit(solution)/shard_map/ppermute | solution.py:28
  58.4 3.5 all-to-all-start.1
  61.9 13.0 %attend.1 = (bf16[336,768]{1,0:T(8,128)(2,1)}, bf16[12,224,256]{2,1,0:T(8,128)(2,1)}, bf16[12,112,256]{2,1,0:T(8,128)(2,1)}) custom-call(s32[8]{0:T(128)} %stack.106.at, bf16[336,2304]{1,0:T(8,128)(2,1)} %fusion.4.q.k.v, bf16[336,2304]{1,0:T(8,128)(2,1)} %fusion.4.q.k.v, bf16[336,2304]{1,0:T(8,128)(2,1)} %fusion.4.q.k.v, f32[768]{0:T(1024)} %v_pad.3, ...), custom_call_target="tpu_custom_call" | custom-call | tf_op jit(solution)/shard_map/attend/pallas_call | solution.py:722
  89.4 4.6 %all-to-all-start.2 = ((f32[32,8,128]{2,1,0:T(8,128)}), f32[32,8,128]{2,1,0:T(8,128)S(1)}, u32[]{:S(2)}, u32[]{:S(2)}) async-start(f32[32,8,128]{2,1,0:T(8,128)} %broadcast_in_dim.76), calls=%async_computation.2 | async-start | bytes 262144 | tf_op jit(solution)/shard_map/all_to_all | solution.py:454
  94.1 6.5 %fusion.3 = (f32[336,3072]{1,0:T(8,128)}, bf16[336,3072]{1,0:T(8,128)(2,1)}) fusion(f32[3072]{0:T(1024)} %param.45, bf16[336,768]{1,0:T(8,128)(2,1)} %add_convert_fusion.2, bf16[768,3072]{1,0:T(8,128)(2,1)} %pad_maximum_fusion), kind=kOutput, calls=%fused_computation.9 | convolution fusion | flops 1596801024 | bytes 11440128 | tf_op jit(solution)/shard_map/dot_general | solution.py:784
  100.6 6.7 %all-to-all-done.2 = f32[32,8,128]{2,1,0:T(8,128)S(1)} async-done(((f32[32,8,128]{2,1,0:T(8,128)}), f32[32,8,128]{2,1,0:T(8,128)S(1)}, u32[]{:S(2)}, u32[]{:S(2)}) %all-to-all-start.2) | async-done | bytes 131104 | tf_op jit(solution)/shard_map/all_to_all | solution.py:454
  108.2 3.5 window.3
  142.2 5.0 %fusion.88 = f32[336,768]{1,0:T(8,128)S(1)} fusion(bf16[336,3072]{1,0:T(8,128)(2,1)S(1)} %multiply_convert_fusion, bf16[768,3072]{1,0:T(8,128)(2,1)} %pad_maximum_fusion), kind=kOutput, calls=%fused_computation.226 | convolution fusion | flops 1585446912 | bytes 7815168 | tf_op jit(solution)/shard_map/dot_general | solution.py:788
  149.9 9.7 %multiply_reduce_fusion = (f32[768]{0:T(1024)}, f32[336]{0:T(512)S(1)}, f32[336]{0:T(512)S(1)}, f32[768]{0:T(1024)}) fusion(f32[336,768]{1,0:T(8,128)S(1)} %fusion.88, f32[336,768]{1,0:T(8,128)S(1)} %get-tuple-element.411, f32[336]{0:T(512)S(1)} %add_rsqrt_fusion.1, f32[336]{0:T(512)S(1)} %broadcast_multiply_fusion.5, f32[768]{0:T(1024)S(1)} %copy-done.54), kind=kLoop, calls=%fused_computation.77 | loop fusion | flops 2320224 | bytes 2078976 | tf_op jit(solution)/shard_map/reduce_sum | solution.py:922
  166.5 18.3 %attend_back.1 = (bf16[336,2304]{1,0:T(8,128)(2,1)}, f32[1,768]{1,0:T(1,128)}, f32[27,64]{1,0:T(8,128)}, f32[27,64]{1,0:T(8,128)}) custom-call(s32[8]{0:T(128)} %stack.106.at, bf16[336,2304]{1,0:T(8,128)(2,1)} %fusion.4.q.k.v, bf16[336,2304]{1,0:T(8,128)(2,1)} %fusion.4.q.k.v, bf16[336,2304]{1,0:T(8,128)(2,1)} %fusion.4.q.k.v, f32[768]{0:T(1024)} %v_pad.3, ...), custom_call_target="tpu_custom_call" | custom-call | tf_op jit(solution)/shard_map/attend_back/pallas_call | solution.py:741
  203.5 4.0 %fusion.11 = f32[336,768]{1,0:T(8,128)S(1)} fusion(bf16[336,2304]{1,0:T(8,128)(2,1)} %get-tuple-element.253, bf16[384,2304]{1,0:T(8,128)(2,1)} %copy-done.26, bf16[384,2304]{1,0:T(8,128)(2,1)} %copy-done.25, pred[336]{0:T(512)(128)(4,1)S(1)} %copy-done.64), kind=kOutput, calls=%fused_computation.49 | convolution fusion | flops 1196421120 | bytes 6119760 | tf_op jit(solution)/shard_map/dot_general | solution.py:788
  230.1 3.9 %unwindow.1 = (bf16[2,8,24,768]{3,2,1,0:T(8,128)(2,1)}, bf16[2,16,24,768]{3,2,1,0:T(8,128)(2,1)}) custom-call(s32[8]{0:T(128)} %stack.106.at, f32[336,768]{1,0:T(8,128)} %get-tuple-element.381.refs_0_, f32[336,768]{1,0:T(8,128)} %fusion.29.refs_1_, bf16[112,192]{1,0:T(8,128)(2,1)} %constant.741.clone.turn.refs_2_), custom_call_target="tpu_custom_call" | custom-call | tf_op jit(solution)/shard_map/unwindow/pallas_call | solution.py:207
  257.8 3.5 all-to-all-start.4
  261.3 4.4 %collective-permute-start.36 = (bf16[48,1920]{1,0:T(8,128)(2,1)}, bf16[48,1920]{1,0:T(8,128)(2,1)}, u32[]{:S(2)}, u32[]{:S(2)}) collective-permute-start(bf16[48,1920]{1,0:T(8,128)(2,1)} %get-tuple-element.285), channel_id=1, source_target_pairs={{0,12},{4,8},{8,4},{12,0},{1,13},{5,9},{9,5},{13,1},{2,14},{6,10},... | collective-permute-start | bytes 552968 | tf_op jit(solution)/shard_map/ppermute | solution.py:374
  269.0 12.9 %collective-permute-done.37 = bf16[2,48,1152]{2,1,0:T(8,128)(2,1)S(1)} collective-permute-done((bf16[2,48,1152]{2,1,0:T(8,128)(2,1)}, bf16[2,48,1152]{2,1,0:T(8,128)(2,1)S(1)}, u32[]{:S(2)}, u32[]{:S(2)}) %collective-permute-start.37) | collective-permute-done | bytes 221216 | tf_op jit(solution)/shard_map/ppermute | solution.py:28
  308.9 5.6 %collective-permute-done.45 = bf16[48,1152]{1,0:T(8,128)(2,1)S(1)} collective-permute-done((bf16[48,1152]{1,0:T(8,128)(2,1)S(1)}, bf16[48,1152]{1,0:T(8,128)(2,1)S(1)}, u32[]{:S(2)}, u32[]{:S(2)}) %collective-permute-start.45) | collective-permute-done | bytes 110624 | tf_op jit(solution)/shard_map/ppermute | solution.py:374
  317.1 11.2 %collective-permute-done.42 = bf16[48,1920]{1,0:T(8,128)(2,1)S(1)} collective-permute-done((bf16[48,1920]{1,0:T(8,128)(2,1)S(1)}, bf16[48,1920]{1,0:T(8,128)(2,1)S(1)}, u32[]{:S(2)}, u32[]{:S(2)}) %collective-permute-start.42) | collective-permute-done | bytes 184352 | tf_op jit(solution)/shard_map/ppermute | solution.py:374
  330.6 4.4 %collective-permute-start.49 = (bf16[48,1152]{1,0:T(8,128)(2,1)S(1)}, bf16[48,1152]{1,0:T(8,128)(2,1)}, u32[]{:S(2)}, u32[]{:S(2)}) collective-permute-start(bf16[48,1152]{1,0:T(8,128)(2,1)S(1)} %add_convert_fusion.8), channel_id=1, source_target_pairs={{0,4},{4,0},{8,12},{12,8},{1,5},{5,1},{9,13},{13,9},{2,6},{6,2},{1... | collective-permute-start | bytes 331784 | tf_op jit(solution)/shard_map/ppermute | solution.py:374
  337.4 11.3 %all_to_all.38 = f32[32,1,397]{2,1,0:T(1,128)S(1)} all-to-all(f32[32,1,397]{2,1,0:T(1,128)S(1)} %broadcast_in_dim.82), channel_id=1, replica_groups=mesh['img'=2,'tok'=4,'yy'=2,'core'=2] {'img','tok','yy','core'}, dimensions={0} | all-to-all | bytes 101632 | tf_op jit(solution)/shard_map/all_to_all | solution.py:460
  349.5 4.7 %final.3 = f32[2,4,192,768]{3,2,1,0:T(8,128)} custom-call(s32[8]{0:T(128)} %stack.106.at, bf16[4,192,384]{2,1,0:T(8,128)(2,1)} %copy-done.18, bf16[4,192,384]{2,1,0:T(8,128)(2,1)} %copy-done.42, bf16[4,192,384]{2,1,0:T(8,128)(2,1)} %copy-done.41, bf16[4,192,384]{2,1,0:T(8,128)(2,1)} %collective-permute-done.47.far_other), custom_call_target="tpu_custom_call" | custom-call | tf_op jit(solution)/shard_map/final/pallas_call | solution.py:418
  361.9 5.3 %final.4 = (f32[2,4,48,3072]{3,2,1,0:T(8,128)}, f32[2,4,48,768]{3,2,1,0:T(8,128)}) custom-call(s32[8]{0:T(128)} %stack.106.at, bf16[4,48,1920]{2,1,0:T(8,128)(2,1)} %copy-done.16, bf16[4,48,1920]{2,1,0:T(8,128)(2,1)} %copy-done.37, bf16[4,48,1920]{2,1,0:T(8,128)(2,1)} %copy-done.36, bf16[4,48,1920]{2,1,0:T(8,128)(2,1)} %copy-done.38), custom_call_target="tpu_custom_call" | custom-call | tf_op jit(solution)/shard_map/final/pallas_call | solution.py:418
  371.7 4.1 %final.5 = f32[2,4,48,2304]{3,2,1,0:T(8,128)} custom-call(s32[8]{0:T(128)} %stack.106.at, bf16[4,48,1152]{2,1,0:T(8,128)(2,1)} %copy-done.27, bf16[4,48,1152]{2,1,0:T(8,128)(2,1)} %collective-permute-done.52.near_other, bf16[4,48,1152]{2,1,0:T(8,128)(2,1)} %collective-permute-done.53.far_own, bf16[4,48,1152]{2,1,0:T(8,128)(2,1)} %copy-done.50), custom_call_target="tpu_custom_call" | custom-call | tf_op jit(solution)/shard_map/final/pallas_call | solution.py:418
  (378 shorter events, 211.3 us)
Async XLA Ops:
  35.4 22.4 %collective-permute-start.7 = (bf16[96,3072]{1,0:T(8,128)(2,1)}, bf16[96,3072]{1,0:T(8,128)(2,1)}, u32[]{:S(2)}, u32[]{:S(2)}) collective-permute-start(bf16[96,3072]{1,0:T(8,128)(2,1)} %get-tuple-element.362), channel_id=1, source_target_pairs={{0,16},{16,0},{1,17},{17,1},{2,18},{18,2},{3,19},{19,3},{4,20},{20... | collective-permute-start | bytes 1769480 | tf_op jit(solution)/shard_map/ppermute | solution.py:28
  38.2 38.0 %collective-permute-start.10 = (bf16[384,768]{1,0:T(8,128)(2,1)}, bf16[384,768]{1,0:T(8,128)(2,1)S(1)}, u32[]{:S(2)}, u32[]{:S(2)}) collective-permute-start(bf16[384,768]{1,0:T(8,128)(2,1)} %get-tuple-element.361), channel_id=1, source_target_pairs={{0,16},{16,0},{1,17},{17,1},{2,18},{18,2},{3,19},{19,3},{4,20},{20... | collective-permute-start | bytes 1769480 | tf_op jit(solution)/shard_map/ppermute | solution.py:28
  38.6 62.0 %collective-permute-start.12 = (bf16[384,768]{1,0:T(8,128)(2,1)}, bf16[384,768]{1,0:T(8,128)(2,1)}, u32[]{:S(2)}, u32[]{:S(2)}) collective-permute-start(bf16[384,768]{1,0:T(8,128)(2,1)} %get-tuple-element.360), channel_id=1, source_target_pairs={{0,16},{16,0},{1,17},{17,1},{2,18},{18,2},{3,19},{19,3},{4,20},{20... | collective-permute-start | bytes 1769480 | tf_op jit(solution)/shard_map/ppermute | solution.py:28
  58.4 27.4 %all-to-all-start.1 = ((bf16[4,2,4,24,768]{4,3,2,1,0:T(8,128)(2,1)}), bf16[4,2,4,24,768]{4,3,2,1,0:T(8,128)(2,1)S(1)}, u32[]{:S(2)}, u32[]{:S(2)}) async-start(bf16[4,2,4,24,768]{4,3,2,1,0:T(8,128)(2,1)} %pack.3), calls=%async_computation.1 | async-start | bytes 2359296 | tf_op jit(solution)/shard_map/all_to_all | solution.py:249
  85.9 21.5 %collective-permute-start.11 = (bf16[2,8,24,768]{3,2,1,0:T(8,128)(2,1)S(1)}, bf16[2,8,24,768]{3,2,1,0:T(8,128)(2,1)}, u32[]{:S(2)}, u32[]{:S(2)}) collective-permute-start(bf16[2,8,24,768]{3,2,1,0:T(8,128)(2,1)S(1)} %bitcast.206), channel_id=1, source_target_pairs={{0,4},{4,8},{8,12},{12,0},{1,5},{5,9},{9,13},{13,1},{2,6},{6,10},{... | collective-permute-start | bytes 1769480 | tf_op jit(solution)/shard_map/ppermute | solution.py:32
  138.4 46.4 %collective-permute-start.18 = (bf16[2,4,192,384]{3,2,1,0:T(8,128)(2,1)}, bf16[2,4,192,384]{3,2,1,0:T(8,128)(2,1)}, u32[]{:S(2)}, u32[]{:S(2)}) collective-permute-start(bf16[2,4,192,384]{3,2,1,0:T(8,128)(2,1)} %fusion.17), channel_id=1, source_target_pairs={{0,16},{16,0},{1,17},{17,1},{2,18},{18,2},{3,19},{19,3},{4,20},{20... | collective-permute-start | bytes 3538952 | tf_op jit(solution)/shard_map/ppermute | solution.py:28
  159.7 28.0 %collective-permute-start.19 = (bf16[2,4,48,1536]{3,2,1,0:T(8,128)(2,1)}, bf16[2,4,48,1536]{3,2,1,0:T(8,128)(2,1)}, u32[]{:S(2)}, u32[]{:S(2)}) collective-permute-start(bf16[2,4,48,1536]{3,2,1,0:T(8,128)(2,1)} %fusion.18), channel_id=1, source_target_pairs={{0,2},{2,0},{1,3},{3,1},{4,6},{6,4},{5,7},{7,5},{8,10},{10,8},{9,1... | collective-permute-start | bytes 3538952 | tf_op jit(solution)/shard_map/ppermute | solution.py:28
  199.7 35.2 %collective-permute-start.24 = (bf16[4,192,384]{2,1,0:T(8,128)(2,1)}, bf16[4,192,384]{2,1,0:T(8,128)(2,1)}, u32[]{:S(2)}, u32[]{:S(2)}) collective-permute-start(bf16[4,192,384]{2,1,0:T(8,128)(2,1)} %fusion.24), channel_id=1, source_target_pairs={{0,2},{2,0},{1,3},{3,1},{4,6},{6,4},{5,7},{7,5},{8,10},{10,8},{9,1... | collective-permute-start | bytes 1769480 | tf_op jit(solution)/shard_map/ppermute | solution.py:28
  200.3 41.0 %collective-permute-start.20 = (bf16[4,48,1536]{2,1,0:T(8,128)(2,1)}, bf16[4,48,1536]{2,1,0:T(8,128)(2,1)}, u32[]{:S(2)}, u32[]{:S(2)}) collective-permute-start(bf16[4,48,1536]{2,1,0:T(8,128)(2,1)} %fusion.23), channel_id=1, source_target_pairs={{0,16},{16,0},{1,17},{17,1},{2,18},{18,2},{3,19},{19,3},{4,20},{20... | collective-permute-start | bytes 1769480 | tf_op jit(solution)/shard_map/ppermute | solution.py:28
  229.6 20.1 %collective-permute-start.30 = (bf16[2,2,48,1152]{3,2,1,0:T(8,128)(2,1)}, bf16[2,2,48,1152]{3,2,1,0:T(8,128)(2,1)}, u32[]{:S(2)}, u32[]{:S(2)}) collective-permute-start(bf16[2,2,48,1152]{3,2,1,0:T(8,128)(2,1)} %fusion.37), channel_id=1, source_target_pairs={{0,2},{2,0},{1,3},{3,1},{4,6},{6,4},{5,7},{7,5},{8,10},{10,8},{9,1... | collective-permute-start | bytes 1327112 | tf_op jit(solution)/shard_map/ppermute | solution.py:28
  241.3 20.1 %collective-permute-start.25 = (bf16[192,384]{1,0:T(8,128)(2,1)}, bf16[192,384]{1,0:T(8,128)(2,1)}, u32[]{:S(2)}, u32[]{:S(2)}) collective-permute-start(bf16[192,384]{1,0:T(8,128)(2,1)} %get-tuple-element.272), channel_id=1, source_target_pairs={{0,4},{4,0},{8,12},{12,8},{1,5},{5,1},{9,13},{13,9},{2,6},{6,2},{1... | collective-permute-start | bytes 442376 | tf_op jit(solution)/shard_map/ppermute | solution.py:374
  241.3 24.5 %collective-permute-start.26 = (bf16[192,384]{1,0:T(8,128)(2,1)}, bf16[192,384]{1,0:T(8,128)(2,1)}, u32[]{:S(2)}, u32[]{:S(2)}) collective-permute-start(bf16[192,384]{1,0:T(8,128)(2,1)} %get-tuple-element.273), channel_id=1, source_target_pairs={{0,8},{4,12},{8,0},{12,4},{1,9},{5,13},{9,1},{13,5},{2,10},{6,14},... | collective-permute-start | bytes 442376 | tf_op jit(solution)/shard_map/ppermute | solution.py:374
  246.4 20.9 %collective-permute-start.27 = (bf16[192,384]{1,0:T(8,128)(2,1)}, bf16[192,384]{1,0:T(8,128)(2,1)}, u32[]{:S(2)}, u32[]{:S(2)}) collective-permute-start(bf16[192,384]{1,0:T(8,128)(2,1)} %get-tuple-element.274), channel_id=1, source_target_pairs={{0,12},{4,8},{8,4},{12,0},{1,13},{5,9},{9,5},{13,1},{2,14},{6,10},... | collective-permute-start | bytes 442376 | tf_op jit(solution)/shard_map/ppermute | solution.py:374
  249.7 38.2 %collective-permute-start.34 = (bf16[48,1920]{1,0:T(8,128)(2,1)}, bf16[48,1920]{1,0:T(8,128)(2,1)}, u32[]{:S(2)}, u32[]{:S(2)}) collective-permute-start(bf16[48,1920]{1,0:T(8,128)(2,1)} %get-tuple-element.283), channel_id=1, source_target_pairs={{0,4},{4,0},{8,12},{12,8},{1,5},{5,1},{9,13},{13,9},{2,6},{6,2},{1... | collective-permute-start | bytes 552968 | tf_op jit(solution)/shard_map/ppermute | solution.py:374
  256.0 34.3 %collective-permute-start.35 = (bf16[48,1920]{1,0:T(8,128)(2,1)}, bf16[48,1920]{1,0:T(8,128)(2,1)}, u32[]{:S(2)}, u32[]{:S(2)}) collective-permute-start(bf16[48,1920]{1,0:T(8,128)(2,1)} %get-tuple-element.284), channel_id=1, source_target_pairs={{0,8},{4,12},{8,0},{12,4},{1,9},{5,13},{9,1},{13,5},{2,10},{6,14},... | collective-permute-start | bytes 552968 | tf_op jit(solution)/shard_map/ppermute | solution.py:374
  257.8 32.5 %all-to-all-start.4 = ((bf16[4,2,4,24,768]{4,3,2,1,0:T(8,128)(2,1)}), bf16[4,2,4,24,768]{4,3,2,1,0:T(8,128)(2,1)S(1)}, u32[]{:S(2)}, u32[]{:S(2)}) async-start(bf16[4,2,4,24,768]{4,3,2,1,0:T(8,128)(2,1)} %bitcast.184), calls=%async_computation.4 | async-start | bytes 2359296 | tf_op jit(solution)/shard_map/all_to_all | solution.py:249
  261.3 29.0 %collective-permute-start.36 = (bf16[48,1920]{1,0:T(8,128)(2,1)}, bf16[48,1920]{1,0:T(8,128)(2,1)}, u32[]{:S(2)}, u32[]{:S(2)}) collective-permute-start(bf16[48,1920]{1,0:T(8,128)(2,1)} %get-tuple-element.285), channel_id=1, source_target_pairs={{0,12},{4,8},{8,4},{12,0},{1,13},{5,9},{9,5},{13,1},{2,14},{6,10},... | collective-permute-start | bytes 552968 | tf_op jit(solution)/shard_map/ppermute | solution.py:374
  299.5 28.8 %collective-permute-start.39 = (bf16[4,192,384]{2,1,0:T(8,128)(2,1)S(1)}, bf16[4,192,384]{2,1,0:T(8,128)(2,1)S(1)}, u32[]{:S(2)}, u32[]{:S(2)}) collective-permute-start(bf16[4,192,384]{2,1,0:T(8,128)(2,1)S(1)} %pad_maximum_fusion.21.near_own), channel_id=1, source_target_pairs={{0,2},{2,0},{1,3},{3,1},{4,6},{6,4},{5,7},{7,5},{8,10},{10,8},{9,1... | collective-permute-start | bytes 1769480 | tf_op jit(solution)/shard_map/ppermute | solution.py:28
  300.2 28.1 %collective-permute-start.40 = (bf16[4,192,384]{2,1,0:T(8,128)(2,1)S(1)}, bf16[4,192,384]{2,1,0:T(8,128)(2,1)S(1)}, u32[]{:S(2)}, u32[]{:S(2)}) collective-permute-start(bf16[4,192,384]{2,1,0:T(8,128)(2,1)S(1)} %pad_maximum_fusion.21.near_own), channel_id=1, source_target_pairs={{0,1},{1,0},{2,3},{3,2},{4,5},{5,4},{6,7},{7,6},{8,9},{9,8},{10,11... | collective-permute-start | bytes 1769480 | tf_op jit(solution)/shard_map/ppermute | solution.py:28
  328.4 21.0 %collective-permute-start.47 = (bf16[4,192,384]{2,1,0:T(8,128)(2,1)S(1)}, bf16[4,192,384]{2,1,0:T(8,128)(2,1)}, u32[]{:S(2)}, u32[]{:S(2)}) collective-permute-start(bf16[4,192,384]{2,1,0:T(8,128)(2,1)S(1)} %collective-permute-done.39.far_own), channel_id=1, source_target_pairs={{0,1},{1,0},{2,3},{3,2},{4,5},{5,4},{6,7},{7,6},{8,9},{9,8},{10,11... | collective-permute-start | bytes 1769480 | tf_op jit(solution)/shard_map/ppermute | solution.py:28
  329.3 26.0 %collective-permute-start.48 = (bf16[4,48,1920]{2,1,0:T(8,128)(2,1)S(1)}, bf16[4,48,1920]{2,1,0:T(8,128)(2,1)S(1)}, u32[]{:S(2)}, u32[]{:S(2)}) collective-permute-start(bf16[4,48,1920]{2,1,0:T(8,128)(2,1)S(1)} %pad_maximum_fusion.19.near_own), channel_id=1, source_target_pairs={{0,2},{2,0},{1,3},{3,1},{4,6},{6,4},{5,7},{7,5},{8,10},{10,8},{9,1... | collective-permute-start | bytes 2211848 | tf_op jit(solution)/shard_map/ppermute | solution.py:28
  330.6 23.6 %collective-permute-start.49 = (bf16[48,1152]{1,0:T(8,128)(2,1)S(1)}, bf16[48,1152]{1,0:T(8,128)(2,1)}, u32[]{:S(2)}, u32[]{:S(2)}) collective-permute-start(bf16[48,1152]{1,0:T(8,128)(2,1)S(1)} %add_convert_fusion.8), channel_id=1, source_target_pairs={{0,4},{4,0},{8,12},{12,8},{1,5},{5,1},{9,13},{13,9},{2,6},{6,2},{1... | collective-permute-start | bytes 331784 | tf_op jit(solution)/shard_map/ppermute | solution.py:374
  335.0 19.2 %collective-permute-start.50 = (bf16[48,1152]{1,0:T(8,128)(2,1)S(1)}, bf16[48,1152]{1,0:T(8,128)(2,1)}, u32[]{:S(2)}, u32[]{:S(2)}) collective-permute-start(bf16[48,1152]{1,0:T(8,128)(2,1)S(1)} %add_convert_fusion.8), channel_id=1, source_target_pairs={{0,8},{4,12},{8,0},{12,4},{1,9},{5,13},{9,1},{13,5},{2,10},{6,14},... | collective-permute-start | bytes 331784 | tf_op jit(solution)/shard_map/ppermute | solution.py:374
  335.1 19.2 %collective-permute-start.51 = (bf16[48,1152]{1,0:T(8,128)(2,1)S(1)}, bf16[48,1152]{1,0:T(8,128)(2,1)}, u32[]{:S(2)}, u32[]{:S(2)}) collective-permute-start(bf16[48,1152]{1,0:T(8,128)(2,1)S(1)} %add_convert_fusion.8), channel_id=1, source_target_pairs={{0,12},{4,8},{8,4},{12,0},{1,13},{5,9},{9,5},{13,1},{2,14},{6,10},... | collective-permute-start | bytes 331784 | tf_op jit(solution)/shard_map/ppermute | solution.py:374
  (112 other events, 1027.6 us)
